TPU v7x, 256 devices: a whole 4x4x8 slice. The times are simulated.
256 devices in a mesh: ctx: 64 (over z, x, core), head: 4 (over y).
Axes of the slice: x: 4, y: 4, z: 8, core: 2. Of those that a mesh axis runs over, the one named last changes fastest.
Arguments:
- inputs: bfloat16 [12288, 2048], P('ctx'), may hold values from -6 to 6
- projection: bfloat16 [3, 2048, 1024], P(None, None, 'head'), may hold values from -0.125 to 0.125
- conv_weight: float32 [3, 4, 1024], P(None, None, 'head'), may hold values from -3 to 3
- gate_code: int32 [8, 12288], P('head', 'ctx'), may hold values from 0 to 1023
- beta_code: int32 [8, 12288], P('head', 'ctx'), may hold values from 0 to 1023
- grad_out: bfloat16 [12288, 1024], P('ctx', 'head'), may hold values from -6 to 6
Outputs:
- input_grad: bfloat16 [12288, 2048], P(('ctx', 'head'))
- kernel_grad: float32 [3, 4, 1024], P(None, None, 'head')
All inputs are finite; a program needn't handle non-finite values.
Results may differ from a plain program's by a relative error of at most 0.0068.
The roundings to bfloat16 on the way count: a program that leaves them out, or rounds other values in their place, can miss the bound.
Values may be sent and summed in bfloat16 or wider, within the bound.
No kernel may reach another device: no remote copies, remote signals or barrier semaphores. Data moves between devices by JAX's collectives and lax.ppermute only.
A program may use at most 64 MiB of HBM per device.

v0:
```python
import jax
import jax.numpy as jnp
from jax import lax
from jax.experimental import pallas as pl
from jax.experimental.pallas import tpu as pltpu
from jax.sharding import PartitionSpec as P


DK = 128
KW = 4
BLOCK = 64
XS = 4
LIMIT = 20 * 2**20
SCALE = DK**-0.5
F32 = jnp.float32
BF16 = jnp.bfloat16
HIGHEST = lax.Precision.HIGHEST
NN = (((1,), (0,)), ((), ()))
NT = (((1,), (1,)), ((), ()))
TN = (((0,), (0,)), ((), ()))


def split(a):
    high = a.astype(BF16)
    return high, (a - high.astype(F32)).astype(BF16)


def dot(a, b, dims):
    return lax.dot_general(a, b, dims, preferred_element_type=F32)


def mm(a, b, dims=NN):
    ah, al = split(a)
    bh, bl = split(b)
    return dot(ah, bh, dims) + (dot(ah, bl, dims) + dot(al, bh, dims))


def mm_left(a, b, dims=NN):
    ah, al = split(a)
    return dot(ah, b, dims) + dot(al, b, dims)


def mm_right(a, b, dims=NN):
    bh, bl = split(b)
    return dot(a, bh, dims) + dot(a, bl, dims)


def exact(a, b, dims):
    return lax.dot_general(a, b, dims, precision=HIGHEST, preferred_element_type=F32)


def iotas(rows, cols):
    return (
        lax.broadcasted_iota(jnp.int32, (rows, cols), 0),
        lax.broadcasted_iota(jnp.int32, (rows, cols), 1),
    )


def eye(n):
    r, c = iotas(n, n)
    return (r == c).astype(F32)


def call(kernel, out_shape, scratch=(), smem=0, flops=0, **kw):
    def run(*args):
        specs = [
            pl.BlockSpec(memory_space=pltpu.SMEM if i < smem else pltpu.VMEM)
            for i in range(len(args))
        ]
        return pl.pallas_call(
            kernel,
            out_shape=out_shape,
            in_specs=specs,
            out_specs=jax.tree.map(lambda _: pl.BlockSpec(memory_space=pltpu.VMEM), out_shape),
            scratch_shapes=list(scratch),
            cost_estimate=pl.CostEstimate(
                flops=flops, bytes_accessed=4_000_000, transcendentals=0
            ),
            compiler_params=pltpu.CompilerParams(vmem_limit_bytes=LIMIT),
            **kw,
        )(*args)

    return run


def shape(s, d=F32):
    return jax.ShapeDtypeStruct(s, d)


def project_kernel(x_ref, w_ref, o_ref, tail_ref):
    value = dot(x_ref[...], w_ref[0], NN).astype(BF16)
    o_ref[0] = value
    rows = value.shape[0]
    tail_ref[0] = value[rows - 16 :].astype(F32)[8:]


def sigmoid(z):
    return 1.0 / (1.0 + jnp.exp(-z))


def local_kernel(
    me_ref, proj_ref, halo_ref, cw_ref, gate_ref, beta_ref, grad_ref,
    keep_ref, send_ref, z_ref, q_ref, k_ref, w_ref, u_ref, p_ref, d_ref, a_ref, t_ref, col_ref,
    ext, buf,
):
    rows = proj_ref.shape[1]
    blocks = rows // BLOCK
    for m in range(3):
        ext[m, 0:8] = halo_ref[m]
        ext[m, 8 : 8 + rows] = proj_ref[m].astype(F32)
    act = []
    for m in range(3):
        z = cw_ref[m, 0:1] * ext[m, 5 : 5 + rows]
        for j in range(1, KW):
            z = z + cw_ref[m, j : j + 1] * ext[m, 5 + j : 5 + j + rows]
        z_ref[m] = z
        act.append(z * sigmoid(z))
    logs = jnp.log(1.0 - 0.001 * gate_ref[...].astype(F32) / 1023.0)
    beta = beta_ref[...].astype(F32) / 1023.0
    r, c = iotas(rows, rows)
    tri = (r >= c).astype(F32)
    col = exact(tri, logs, NT)
    row = exact(logs, tri, NT)
    betas = exact((r == c).astype(F32), beta, NT)
    r64, c64 = iotas(BLOCK, BLOCK)
    diag = []
    keys = []
    queries = []
    for h in range(2):
        lanes = slice(h * DK, (h + 1) * DK)
        aq = act[0][:, lanes]
        ak = act[1][:, lanes]
        queries.append(aq * lax.rsqrt(jnp.sum(aq * aq, -1, keepdims=True) + 1e-06) * SCALE)
        keys.append(ak * lax.rsqrt(jnp.sum(ak * ak, -1, keepdims=True) + 1e-06))
        b = col[:, h : h + 1]
        bt = betas[:, h : h + 1]
        decay = jnp.where(r >= c, jnp.exp(b - row[h : h + 1]), 0.0)
        d_ref[h] = decay
        gram = mm(keys[h], keys[h], NT)
        a_ref[h] = jnp.where(r > c, decay * gram * bt, 0.0)
        p_ref[h] = decay * mm(queries[h], keys[h], NT)
        q_ref[h] = queries[h]
        k_ref[h] = keys[h]
        total = col[rows - 1 : rows, h : h + 1]
        col_ref[h, 0] = jnp.broadcast_to(jnp.exp(b), (rows, DK))
        col_ref[h, 1] = jnp.broadcast_to(bt, (rows, DK))
        col_ref[h, 2] = jnp.broadcast_to(jnp.exp(total - b), (rows, DK))
        for i in range(blocks):
            span = slice(i * BLOCK, (i + 1) * BLOCK)
            kb = keys[h][span]
            rb = exact(logs, tri[span], NT)[h : h + 1]
            dec = jnp.exp(b[span] - rb)
            diag.append(jnp.where(r64 > c64, dec * mm(kb, kb, NT) * bt[span], 0.0))
    lower = jnp.stack(diag)
    count = len(diag)
    tiles = []
    for k in range(BLOCK // 8):
        rr = lax.broadcasted_iota(jnp.int32, (count, 8, BLOCK), 1) + 8 * k
        cc = lax.broadcasted_iota(jnp.int32, (count, 8, BLOCK), 2)
        tiles.append((rr == cc).astype(F32))
    for s in range(BLOCK - 1):
        k0, r0 = divmod(s, 8)
        pivot = tiles[k0][:, r0 : r0 + 1, :]
        for k in range(k0, BLOCK // 8):
            tiles[k] = tiles[k] - lower[:, 8 * k : 8 * k + 8, s : s + 1] * pivot
    inverse = jnp.concatenate(tiles, 1)
    for h in range(2):
        for i in range(blocks):
            t_ref[h, i] = inverse[h * blocks + i]
    for h in range(2):
        lanes = slice(h * DK, (h + 1) * DK)
        eb = col_ref[h, 0]
        bt = col_ref[h, 1]
        rest = col_ref[h, 2]
        rhs = jnp.concatenate([bt * eb * keys[h], bt * act[2][:, lanes]], 1)
        done = []
        for i in range(blocks):
            span = slice(i * BLOCK, (i + 1) * BLOCK)
            part = rhs[span]
            if i > 0:
                past = jnp.concatenate(done, 0) if i > 1 else done[0]
                part = part - mm(a_ref[h, span, 0 : i * BLOCK], past)
            done.append(mm(inverse[h * blocks + i], part))
        wu = jnp.concatenate(done, 0)
        w = wu[:, :DK]
        w_ref[h] = w
        u_ref[h] = wu[:, DK:]
        kt = rest * keys[h]
        ml = mm(wu, kt, TN)
        buf[h, 0] = eb[rows - 1 : rows] * eye(DK) - ml[:DK]
        buf[h, 1] = ml[DK:]
        effective = eb * queries[h] - mm(p_ref[h], w)
        buf[h, 2] = mm_right(grad_ref[:, lanes], effective, TN)
    core = me_ref[0]
    keep_ref[...] = buf[core]
    send_ref[...] = buf[1 - core]


def adjoint_kernel(p_ref, a_ref, t_ref, k_ref, col_ref, grad_ref, dr_ref, e_ref):
    rows = k_ref.shape[1]
    blocks = rows // BLOCK
    for h in range(2):
        lanes = slice(h * DK, (h + 1) * DK)
        back = mm_left(p_ref[h], grad_ref[:, lanes], TN)
        rhs = jnp.concatenate([back, col_ref[h, 2] * k_ref[h]], 1)
        done = {}
        for i in reversed(range(blocks)):
            span = slice(i * BLOCK, (i + 1) * BLOCK)
            part = rhs[span]
            for j in range(i + 1, blocks):
                below = slice(j * BLOCK, (j + 1) * BLOCK)
                wide = mm(a_ref[h, below], done[j], TN)
                part = part - wide[span]
            done[i] = mm(t_ref[h, i], part, TN)
        full = jnp.concatenate([done[i] for i in range(blocks)], 0)
        dr_ref[h] = full[:, :DK]
        e_ref[h] = full[:, DK:]


def ordered_pair(me_ref, keep_ref, recv_ref):
    first = me_ref[0] == 0
    keep, recv = keep_ref[...], recv_ref[...]
    return jnp.where(first, keep, recv), jnp.where(first, recv, keep)


def pair_kernel(me_ref, keep_ref, recv_ref, out_ref):
    e0, e1 = ordered_pair(me_ref, keep_ref, recv_ref)
    both = mm(jnp.concatenate([e0[0], e0[1]], 0), e1[0])
    out_ref[0] = (both[:DK] - eye(DK)).astype(BF16)
    out_ref[1] = (both[DK:] + e1[1]).astype(BF16)
    out_ref[2] = (mm(e1[2], e0[0], NT) + e0[2]).astype(BF16)


def group_kernel(me_ref, own_ref, r1, r2, r3, pre_ref, suf_ref, out_ref, el):
    x = me_ref[1]
    one = eye(DK)
    zero = jnp.zeros((DK, DK), F32)
    for k, ref in enumerate((own_ref, r1, r2, r3)):
        el[lax.rem(x + XS - k, XS)] = ref[...]

    def put(ref, value):
        ref[0] = value[:DK]
        ref[1] = value[DK:]

    start = jnp.concatenate([one, zero], 0)
    fwd = start
    bwd = start
    for j in range(XS):

        @pl.when(x == j)
        def _(fwd=fwd):
            put(pre_ref, fwd)

        @pl.when(x == XS - 1 - j)
        def _(bwd=bwd):
            put(suf_ref, bwd)

        mf = el[j, 0]
        mb = el[XS - 1 - j, 0]
        lf = el[j, 1].astype(F32)
        gb = el[XS - 1 - j, 2].astype(F32)
        if j == 0:
            fwd = jnp.concatenate([one + mf.astype(F32), lf], 0)
            bwd = jnp.concatenate([one + mb.astype(F32).T, gb], 0)
        else:
            fwd = fwd + mm_left(fwd, mf, NN) + jnp.concatenate([zero, lf], 0)
            bwd = bwd + mm_left(bwd, mb, NT) + jnp.concatenate([zero, gb], 0)
    out_ref[0] = (fwd[:DK] - one).astype(BF16)
    out_ref[1] = fwd[DK:].astype(BF16)
    out_ref[2] = bwd[DK:].astype(BF16)


def merge_kernel(me_ref, own_ref, recv_ref, o1, o2, o3):
    first = lax.rem(me_ref[2], 2) == 0
    pair = me_ref[2] // 2
    own, recv = own_ref[...], recv_ref[...]
    e0 = jnp.where(first, own, recv)
    e1 = jnp.where(first, recv, own)
    both = dot(jnp.concatenate([e0[0], e0[1]], 0), e1[0], NN)
    m = e0[0].astype(F32) + e1[0].astype(F32) + both[:DK]
    s = e0[1].astype(F32) + e1[1].astype(F32) + both[DK:]
    g = e0[2].astype(F32) + e1[2].astype(F32) + dot(e1[2], e0[0], NT)
    m = m.astype(BF16)
    for k, ref in ((1, o1), (2, o2), (3, o3)):
        ref[0] = m
        ref[1] = jnp.where(pair + k < 4, s, g).astype(BF16)


def enter_kernel(
    me_ref, r1, r2, r3, near_ref, pre_ref, suf_ref, keep_ref, recv_ref, own_ref, send_ref
):
    z = me_ref[2]
    pair = z // 2
    first = lax.rem(z, 2) == 0
    s = jnp.zeros((DK, DK), F32)
    g = jnp.zeros((DK, DK), F32)
    for k, ref in ((3, r3), (2, r2), (1, r1)):
        add = ref[1].astype(F32)
        new = add if k == 3 else s + mm_left(s, ref[0], NN) + add
        s = jnp.where(k <= pair, new, s)
    for k, ref in ((1, r1), (2, r2), (3, r3)):
        add = ref[1].astype(F32)
        new = add if k == 1 else g + mm_left(g, ref[0], NT) + add
        g = jnp.where(k > pair, new, g)
    near = near_ref[0]
    s = jnp.where(first, s, s + mm_left(s, near, NN) + near_ref[1].astype(F32))
    g = jnp.where(first, g + mm_left(g, near, NT) + near_ref[2].astype(F32), g)
    s = mm(s, pre_ref[0]) + pre_ref[1]
    g = mm(g, suf_ref[0]) + suf_ref[1]
    e0, e1 = ordered_pair(me_ref, keep_ref, recv_ref)
    s1 = mm(s, e0[0]) + e0[1]
    g0 = mm(g, e1[0], NT) + e1[2]
    first = me_ref[0] == 0
    own_ref[0] = jnp.where(first, s, s1)
    own_ref[1] = jnp.where(first, g0, g)
    send_ref[0] = jnp.where(first, s1, s)
    send_ref[1] = jnp.where(first, g, g0)


def backward_kernel(
    me_ref, own_ref, recv_ref, proj_ref, halo_ref, cw_ref, grad_ref,
    z_ref, q_ref, k_ref, w_ref, u_ref, d_ref, col_ref, dr_ref, e_ref,
    out_ref, tail_ref, spill_ref, taps_ref,
    ext, dzs,
):
    rows = proj_ref.shape[1]
    core = me_ref[0]
    r, c = iotas(rows, rows)
    pads = jnp.zeros((8, dzs.shape[2]), F32)
    for m in range(3):
        ext[m, 0:8] = halo_ref[m]
        ext[m, 8 : 8 + rows] = proj_ref[m].astype(F32)
        dzs[m, 0:8] = pads
        dzs[m, 8 + rows : 16 + rows] = pads
    for h in range(2):
        lanes = slice(h * DK, (h + 1) * DK)
        mine = core == h
        s = jnp.where(mine, own_ref[0], recv_ref[0])
        g = jnp.where(mine, own_ref[1], recv_ref[1])
        q, k = q_ref[h], k_ref[h]
        eb, bt, rest = col_ref[h, 0], col_ref[h, 1], col_ref[h, 2]
        do = grad_ref[:, lanes].astype(F32)
        u = u_ref[h] - mm(w_ref[h], s, NT)
        dr = dr_ref[h] + mm(e_ref[h], g, NT)
        cross = mm(jnp.concatenate([do, dr], 0), u, NT)
        decay = d_ref[h]
        x1 = decay * cross[:rows]
        da = jnp.where(r > c, decay * cross[rows:], 0.0) * -bt[:, :1]
        outer = mm(jnp.concatenate([eb * do, -(bt * eb) * dr], 0), s)
        right = mm(jnp.concatenate([x1, da], 0), k)
        dq = outer[:rows] + right[:rows]
        dk = outer[rows:] + right[rows:] + rest * mm(u, g)
        dk = dk + mm(jnp.concatenate([x1, da], 0), jnp.concatenate([q, k], 0), TN)
        dv = bt * dr
        zq = z_ref[0, :, lanes]
        zk = z_ref[1, :, lanes]
        zv = z_ref[2, :, lanes]
        sq, sk, sv = sigmoid(zq), sigmoid(zk), sigmoid(zv)
        aq, ak = zq * sq, zk * sk
        rq = lax.rsqrt(jnp.sum(aq * aq, -1, keepdims=True) + 1e-06)
        rk = lax.rsqrt(jnp.sum(ak * ak, -1, keepdims=True) + 1e-06)
        daq = rq * (SCALE * dq - q * (jnp.sum(q * dq, -1, keepdims=True) * (1.0 / SCALE)))
        dak = rk * (dk - k * jnp.sum(k * dk, -1, keepdims=True))
        dzs[0, 8 : 8 + rows, lanes] = daq * (sq * (1.0 + zq * (1.0 - sq)))
        dzs[1, 8 : 8 + rows, lanes] = dak * (sk * (1.0 + zk * (1.0 - sk)))
        dzs[2, 8 : 8 + rows, lanes] = dv * (sv * (1.0 + zv * (1.0 - sv)))
    for m in range(3):
        dz = dzs[m, 8 : 8 + rows]
        dx = None
        spill = None
        for j in range(KW):
            tap = cw_ref[m, j : j + 1]
            term = tap * dzs[m, 11 - j : 11 - j + rows]
            first = tap * dzs[m, 3 - j : 11 - j]
            dx = term if dx is None else dx + term
            spill = first if spill is None else spill + first
            taps_ref[m, j : j + 1] = jnp.sum(dz * ext[m, 5 + j : 5 + j + rows], 0, keepdims=True)
        out_ref[m] = dx.astype(BF16)
        tail_ref[m] = dx[rows - 16 :]
        spill_ref[m] = spill


def output_kernel(me_ref, grad_ref, tail_ref, spill_ref, w_ref, o0, o1, o2, o3, lhs, fixed):
    rows = grad_ref.shape[1]
    part = rows // 4

    @pl.when(pl.program_id(0) == 0)
    def _():
        fixed[...] = grad_ref[...]
        for m in range(3):
            add = jnp.concatenate([jnp.zeros((8, spill_ref.shape[2]), F32), spill_ref[m]], 0)
            fixed[m, rows - 16 :] = (tail_ref[m] + add).astype(BF16)
        for k in range(4):
            at = pl.multiple_of(lax.rem(me_ref[3] + k, 4) * part, part)
            for m in range(3):
                lhs[m, k * part : (k + 1) * part] = fixed[m, pl.ds(at, part)]

    total = dot(lhs[0], w_ref[0], NT) + dot(lhs[1], w_ref[1], NT) + dot(lhs[2], w_ref[2], NT)
    o0[...] = total[:part]
    for k, ref in ((1, o1), (2, o2), (3, o3)):
        ref[...] = total[k * part : (k + 1) * part].astype(BF16)


def body(inputs, projection, conv_weight, gate_code, beta_code, grad_out):
    n = lax.axis_size("ctx")
    heads = lax.axis_size("head")
    rows, width = inputs.shape
    lanes = projection.shape[2]
    blocks = rows // BLOCK
    at = lax.axis_index("ctx")
    me = jnp.stack([at % 2, (at // 2) % XS, at // (2 * XS), lax.axis_index("head")]).astype(
        jnp.int32
    )

    def swap(block, bit):
        return lax.ppermute(block, "ctx", [(i, i ^ bit) for i in range(n)])

    def turn(block, stride, k):
        route = []
        for i in range(n):
            place = (i // stride) % 4
            route.append((i, i + ((place + k) % 4 - place) * stride))
        return lax.ppermute(block, "ctx", route)


    projected, tail = pl.pallas_call(
        project_kernel,
        grid=(3,),
        in_specs=[
            pl.BlockSpec((rows, width), lambda m: (0, 0)),
            pl.BlockSpec((1, width, lanes), lambda m: (m, 0, 0)),
        ],
        out_specs=(
            pl.BlockSpec((1, rows, lanes), lambda m: (m, 0, 0)),
            pl.BlockSpec((1, 8, lanes), lambda m: (m, 0, 0)),
        ),
        out_shape=(shape((3, rows, lanes), BF16), shape((3, 8, lanes))),
        compiler_params=pltpu.CompilerParams(vmem_limit_bytes=LIMIT),
    )(inputs, projection)
    halo = lax.ppermute(tail, "ctx", [(i, i + 1) for i in range(n - 1)])
    square = (2, rows, rows)
    tall = (2, rows, DK)
    triple = (3, DK, DK)
    keep, send, z, q, k, w, u, p, d, a, t, col = call(
        local_kernel,
        (
            shape(triple), shape(triple), shape((3, rows, lanes)), shape(tall), shape(tall),
            shape(tall), shape(tall), shape(square), shape(square), shape(square),
            shape((2, blocks, BLOCK, BLOCK)), shape((2, 3, rows, DK)),
        ),
        scratch=(pltpu.VMEM((3, rows + 8, lanes), F32), pltpu.VMEM((2, 3, DK, DK), F32)),
        smem=1,
        flops=2_000_000_000,
    )(me, projected, halo, conv_weight, gate_code, beta_code, grad_out)
    recv = swap(send, 1)
    dr, e = call(adjoint_kernel, (shape(tall), shape(tall)), flops=500_000_000)(
        p, a, t, k, col, grad_out
    )
    group = call(pair_kernel, shape(triple, BF16), smem=1)(me, keep, recv)
    pre, suf, whole = call(
        group_kernel,
        (shape((2, DK, DK)), shape((2, DK, DK)), shape(triple, BF16)),
        scratch=(pltpu.VMEM((XS, 3, DK, DK), BF16),),
        smem=1,
    )(me, group, *(turn(group, 2, k) for k in (1, 2, 3)))
    near = swap(whole, 2 * XS)
    far = call(merge_kernel, (shape((2, DK, DK), BF16),) * 3, smem=1)(me, whole, near)
    far = [turn(block, 4 * XS, k) for k, block in enumerate(far, 1)]
    own, other = call(enter_kernel, (shape((2, DK, DK)), shape((2, DK, DK))), smem=1)(
        me, *far, near, pre, suf, keep, recv
    )
    other = swap(other, 1)
    rounded, edge, spill, taps = call(
        backward_kernel,
        (
            shape((3, rows, lanes), BF16), shape((3, 16, lanes)), shape((3, 8, lanes)),
            shape((3, KW, lanes)),
        ),
        scratch=(
            pltpu.VMEM((3, rows + 8, lanes), F32),
            pltpu.VMEM((3, rows + 16, lanes), F32),
        ),
        smem=1,
        flops=2_000_000_000,
    )(me, own, other, projected, halo, conv_weight, grad_out, z, q, k, w, u, d, col, dr, e)
    spill = lax.ppermute(spill, "ctx", [(i + 1, i) for i in range(n - 1)])
    part = rows // heads
    step = 512
    out = pl.BlockSpec((part, step), lambda i: (0, i))
    mine, *sends = pl.pallas_call(
        output_kernel,
        grid=(width // step,),
        in_specs=[
            pl.BlockSpec(memory_space=pltpu.SMEM),
            pl.BlockSpec((3, rows, lanes), lambda i: (0, 0, 0)),
            pl.BlockSpec((3, 16, lanes), lambda i: (0, 0, 0)),
            pl.BlockSpec((3, 8, lanes), lambda i: (0, 0, 0)),
            pl.BlockSpec((3, step, lanes), lambda i: (0, i, 0)),
        ],
        out_specs=(out,) * 4,
        out_shape=(shape((part, width)),) + (shape((part, width), BF16),) * 3,
        scratch_shapes=[pltpu.VMEM((3, rows, lanes), BF16)] * 2,
        compiler_params=pltpu.CompilerParams(vmem_limit_bytes=LIMIT),
        cost_estimate=pl.CostEstimate(
            flops=2 * 3 * rows * lanes * width, bytes_accessed=4_000_000, transcendentals=0
        ),
    )(me, rounded, edge, spill, projection)
    total = mine
    for shift, block in enumerate(sends, 1):
        got = lax.ppermute(block, "head", [(i, (i + shift) % heads) for i in range(heads)])
        total = total + got.astype(F32)

    def around(taps, stride):
        r1, r2, r3 = (turn(taps, stride, k) for k in (1, 2, 3))
        return (taps + r2) + (r1 + r3)

    taps = taps + swap(taps, 1)
    taps = around(taps, 2)
    taps = taps + swap(taps, 2 * XS)
    taps = around(taps, 4 * XS)
    return (total.astype(BF16), taps)


def solution(mesh):
    return jax.shard_map(
        body,
        mesh=mesh,
        in_specs=(
            P("ctx", None),
            P(None, None, "head"),
            P(None, None, "head"),
            P("head", "ctx"),
            P("head", "ctx"),
            P("ctx", "head"),
        ),
        out_specs=(P(("ctx", "head"), None), P(None, None, "head")),
        check_vma=False,
    )
```

profile of v0, /device:TPU:2, one launch (start us, length us, event | category | flops | bytes accessed | tf_op | source)
XLA Modules:
  0.0 93.1 jit_solution(16019432211126852869)
XLA Ops:
  0.6 1.9 %copy-done = bf16[3,2048,256]{2,1,0:T(8,128)(2,1)S(1)} copy-done((bf16[3,2048,256]{2,1,0:T(8,128)(2,1)S(1)}, bf16[3,2048,256]{2,1,0:T(8,128)(2,1)}, u32[]{:S(2)}) %copy-start) | copy-done | bytes 3145752
  3.7 1.2 %shard_map.77 = (bf16[3,192,256]{2,1,0:T(8,128)(2,1)S(1)}, f32[3,8,256]{2,1,0:T(8,128)S(1)}) custom-call(bf16[192,2048]{1,0:T(8,128)(2,1)S(1)} %copy-done.2, bf16[3,2048,256]{2,1,0:T(8,128)(2,1)S(1)} %copy-done), custom_call_target="tpu_custom_call" | custom-call | tf_op jit(solution)/shard_map/pallas_call | solution.py:426
  4.9 1.9 %collective-permute-start = (f32[3,8,256]{2,1,0:T(8,128)S(1)}, f32[3,8,256]{2,1,0:T(8,128)S(1)}, u32[]{:S(2)}, u32[]{:S(2)}) collective-permute-start(f32[3,8,256]{2,1,0:T(8,128)S(1)} %get-tuple-element.35), channel_id=1, source_target_pairs={{0,4},{4,8},{8,12},{12,16},{16,20},{20,24},{24,28},{28,32},{32,36}... | collective-permute-start | bytes 73736 | tf_op jit(solution)/shard_map/ppermute | solution.py:440
  6.9 3.1 %collective-permute-done.halo_ref = f32[3,8,256]{2,1,0:T(8,128)S(1)} collective-permute-done((f32[3,8,256]{2,1,0:T(8,128)S(1)}, f32[3,8,256]{2,1,0:T(8,128)S(1)}, u32[]{:S(2)}, u32[]{:S(2)}) %collective-permute-start) | collective-permute-done | bytes 24608 | tf_op jit(solution)/shard_map/ppermute | solution.py:440
  10.0 5.6 %shard_map.78 = (f32[3,128,128]{2,1,0:T(8,128)S(1)}, f32[3,128,128]{2,1,0:T(8,128)S(1)}, f32[3,192,256]{2,1,0:T(8,128)S(1)}, f32[2,192,128]{2,1,0:T(8,128)S(1)},...) custom-call(s32[4]{0:T(128)S(1)} %pad_add_fusion.me_ref, ...), custom_call_target="tpu_custom_call" | custom-call | flops 2000000000 | bytes 4000000 | tf_op jit(solution)/shard_map/pallas_call | solution.py:70
  15.7 1.4 %collective-permute-done.1.recv_ref = f32[3,128,128]{2,1,0:T(8,128)S(1)} collective-permute-done((f32[3,128,128]{2,1,0:T(8,128)S(1)}, f32[3,128,128]{2,1,0:T(8,128)S(1)}, u32[]{:S(2)}, u32[]{:S(2)}) %collective-permute-start.1) | collective-permute-done | bytes 196640 | tf_op jit(solution)/shard_map/ppermute | solution.py:416
  18.0 1.6 %collective-permute-start.2 = (bf16[3,128,128]{2,1,0:T(8,128)(2,1)S(1)}, bf16[3,128,128]{2,1,0:T(8,128)(2,1)S(1)}, u32[]{:S(2)}, u32[]{:S(2)}) collective-permute-start(bf16[3,128,128]{2,1,0:T(8,128)(2,1)S(1)} %shard_map.79.own_ref), channel_id=1, source_target_pairs={{0,8},{4,12},{8,16},{12,20},{16,24},{20,28},{24,0},{28,4},{32,40},... | collective-permute-start | bytes 294920 | tf_op jit(solution)/shard_map/ppermute | solution.py:423
  20.3 2.5 %collective-permute-start.4 = (bf16[3,128,128]{2,1,0:T(8,128)(2,1)S(1)}, bf16[3,128,128]{2,1,0:T(8,128)(2,1)S(1)}, u32[]{:S(2)}, u32[]{:S(2)}) collective-permute-start(bf16[3,128,128]{2,1,0:T(8,128)(2,1)S(1)} %shard_map.79.own_ref), channel_id=1, source_target_pairs={{0,24},{4,28},{8,0},{12,4},{16,8},{20,12},{24,16},{28,20},{32,56},... | collective-permute-start | bytes 294920 | tf_op jit(solution)/shard_map/ppermute | solution.py:423
  22.9 3.8 %collective-permute-done.3.r2 = bf16[3,128,128]{2,1,0:T(8,128)(2,1)S(1)} collective-permute-done((bf16[3,128,128]{2,1,0:T(8,128)(2,1)S(1)}, bf16[3,128,128]{2,1,0:T(8,128)(2,1)S(1)}, u32[]{:S(2)}, u32[]{:S(2)}) %collective-permute-start.3) | collective-permute-done | bytes 98336 | tf_op jit(solution)/shard_map/ppermute | solution.py:423
  26.9 1.4 %shard_map.80 = (f32[2,128,128]{2,1,0:T(8,128)S(1)}, f32[2,128,128]{2,1,0:T(8,128)S(1)}, bf16[3,128,128]{2,1,0:T(8,128)(2,1)S(1)}) custom-call(s32[4]{0:T(128)S(1)} %pad_add_fusion.me_ref, bf16[3,128,128]{2,1,0:T(8,128)(2,1)S(1)} %shard_map.79.own_ref, bf16[3,128,128]{2,1,0:T(8,128)(2,1)S(1)} %collective-permute-done.2.r1, ...), custom_call_target="tpu_custom_call" | custom-call | bytes 4000000 | tf_op jit(solution)/shard_map/pallas_call | solution.py:70
  28.3 3.0 %collective-permute-start.5 = (bf16[3,128,128]{2,1,0:T(8,128)(2,1)S(1)}, bf16[3,128,128]{2,1,0:T(8,128)(2,1)S(1)}, u32[]{:S(2)}, u32[]{:S(2)}) collective-permute-start(bf16[3,128,128]{2,1,0:T(8,128)(2,1)S(1)} %get-tuple-element.38.own_ref), channel_id=1, source_target_pairs={{0,32},{4,36},{8,40},{12,44},{16,48},{20,52},{24,56},{28,60},{32,0... | collective-permute-start | bytes 294920 | tf_op jit(solution)/shard_map/ppermute | solution.py:416
  31.3 2.6 %collective-permute-done.5.recv_ref.near_ref = bf16[3,128,128]{2,1,0:T(8,128)(2,1)S(1)} collective-permute-done((bf16[3,128,128]{2,1,0:T(8,128)(2,1)S(1)}, bf16[3,128,128]{2,1,0:T(8,128)(2,1)S(1)}, u32[]{:S(2)}, u32[]{:S(2)}) %collective-permute-start.5) | collective-permute-done | bytes 98336 | tf_op jit(solution)/shard_map/ppermute | solution.py:416
  34.6 3.5 %collective-permute-start.6 = (bf16[2,128,128]{2,1,0:T(8,128)(2,1)S(1)}, bf16[2,128,128]{2,1,0:T(8,128)(2,1)S(1)}, u32[]{:S(2)}, u32[]{:S(2)}) collective-permute-start(bf16[2,128,128]{2,1,0:T(8,128)(2,1)S(1)} %get-tuple-element.39), channel_id=1, source_target_pairs={{0,64},{4,68},{8,72},{12,76},{16,80},{20,84},{24,88},{28,92},{32,9... | collective-permute-start | bytes 196616 | tf_op jit(solution)/shard_map/ppermute | solution.py:423
  38.1 5.4 %collective-permute-start.7 = (bf16[2,128,128]{2,1,0:T(8,128)(2,1)S(1)}, bf16[2,128,128]{2,1,0:T(8,128)(2,1)S(1)}, u32[]{:S(2)}, u32[]{:S(2)}) collective-permute-start(bf16[2,128,128]{2,1,0:T(8,128)(2,1)S(1)} %get-tuple-element.40), channel_id=1, source_target_pairs={{0,128},{4,132},{8,136},{12,140},{16,144},{20,148},{24,152},{28,15... | collective-permute-start | bytes 196616 | tf_op jit(solution)/shard_map/ppermute | solution.py:423
  43.5 3.7 %collective-permute-start.8 = (bf16[2,128,128]{2,1,0:T(8,128)(2,1)S(1)}, bf16[2,128,128]{2,1,0:T(8,128)(2,1)S(1)}, u32[]{:S(2)}, u32[]{:S(2)}) collective-permute-start(bf16[2,128,128]{2,1,0:T(8,128)(2,1)S(1)} %get-tuple-element.41), channel_id=1, source_target_pairs={{0,192},{4,196},{8,200},{12,204},{16,208},{20,212},{24,216},{28,22... | collective-permute-start | bytes 196616 | tf_op jit(solution)/shard_map/ppermute | solution.py:423
  47.2 2.3 %collective-permute-done.8.r3 = bf16[2,128,128]{2,1,0:T(8,128)(2,1)S(1)} collective-permute-done((bf16[2,128,128]{2,1,0:T(8,128)(2,1)S(1)}, bf16[2,128,128]{2,1,0:T(8,128)(2,1)S(1)}, u32[]{:S(2)}, u32[]{:S(2)}) %collective-permute-start.8) | collective-permute-done | bytes 65568 | tf_op jit(solution)/shard_map/ppermute | solution.py:423
  49.5 1.4 %shard_map.82 = (f32[2,128,128]{2,1,0:T(8,128)S(1)}, f32[2,128,128]{2,1,0:T(8,128)S(1)}) custom-call(s32[4]{0:T(128)S(1)} %pad_add_fusion.me_ref, bf16[2,128,128]{2,1,0:T(8,128)(2,1)S(1)} %collective-permute-done.6.r1, bf16[2,128,128]{2,1,0:T(8,128)(2,1)S(1)} %collective-permute-done.7.r2, bf16[2,128,128]{2,1,0:T(8,128)(2,1)S(1)} %collective-permute-done.8.r3, ...), custom_call_target="tpu_custom_call" | custom-call | bytes 4000000 | tf_op jit(solution)/shard_map/pallas_call | solution.py:70
  51.2 2.4 %shard_map.83 = (f32[2,192,128]{2,1,0:T(8,128)S(1)}, f32[2,192,128]{2,1,0:T(8,128)S(1)}) custom-call(f32[2,192,192]{2,1,0:T(8,128)S(1)} %get-tuple-element.53.p_ref, f32[2,192,192]{2,1,0:T(8,128)S(1)} %get-tuple-element.54.a_ref, f32[2,3,64,64]{3,2,1,0:T(8,128)S(1)} %get-tuple-element.55.t_ref, f32[2,192,128]{2,1,0:T(8,128)S(1)} %get-tuple-element.48.k_ref, ...), custom_call_target="tpu_custom_call" | custom-call | flops 500000000 | bytes 4000000 | tf_op jit(solution)/shard_map/pallas_call | solution.py:70
  53.6 3.4 %shard_map.84 = (bf16[3,192,256]{2,1,0:T(8,128)(2,1)S(1)}, f32[3,16,256]{2,1,0:T(8,128)S(1)}, f32[3,8,256]{2,1,0:T(8,128)S(1)}, f32[3,4,256]{2,1,0:T(4,128)S(1)}) custom-call(s32[4]{0:T(128)S(1)} %pad_add_fusion.me_ref, f32[2,128,128]{2,1,0:T(8,128)S(1)} %get-tuple-element.44.own_ref, f32[2,128,128]{2,1,0:T(8,128)S(1)} %collective-permute-done.9.recv_ref, ...), custom_call_target="tpu_custom_call" | custom-call | flops 2000000000 | bytes 4000000 | tf_op jit(solution)/shard_map/pallas_call | solution.py:70
  58.4 2.9 %collective-permute-start.15 = (f32[3,4,256]{2,1,0:T(4,128)S(1)}, f32[3,4,256]{2,1,0:T(4,128)S(1)}, u32[]{:S(2)}, u32[]{:S(2)}) collective-permute-start(f32[3,4,256]{2,1,0:T(4,128)S(1)} %add.47), channel_id=1, source_target_pairs={{0,16},{4,20},{8,24},{12,28},{16,0},{20,4},{24,8},{28,12},{32,48},... | collective-permute-start | bytes 36872 | tf_op jit(solution)/shard_map/ppermute | solution.py:423
  61.7 1.6 %collective-permute-start.17 = (f32[3,4,256]{2,1,0:T(4,128)S(1)}, f32[3,4,256]{2,1,0:T(4,128)S(1)}, u32[]{:S(2)}, u32[]{:S(2)}) collective-permute-start(f32[3,4,256]{2,1,0:T(4,128)S(1)} %add.47), channel_id=1, source_target_pairs={{0,24},{4,28},{8,0},{12,4},{16,8},{20,12},{24,16},{28,20},{32,56},... | collective-permute-start | bytes 36872 | tf_op jit(solution)/shard_map/ppermute | solution.py:423
  63.3 1.9 %collective-permute-start.10 = (f32[3,8,256]{2,1,0:T(8,128)S(1)}, f32[3,8,256]{2,1,0:T(8,128)S(1)}, u32[]{:S(2)}, u32[]{:S(2)}) collective-permute-start(f32[3,8,256]{2,1,0:T(8,128)S(1)} %get-tuple-element.60), channel_id=1, source_target_pairs={{4,0},{8,4},{12,8},{16,12},{20,16},{24,20},{28,24},{32,28},{36,32}... | collective-permute-start | bytes 73736 | tf_op jit(solution)/shard_map/ppermute | solution.py:486
  65.8 3.4 %collective-permute-done.18 = f32[3,4,256]{2,1,0:T(4,128)S(1)} collective-permute-done((f32[3,4,256]{2,1,0:T(4,128)S(1)}, f32[3,4,256]{2,1,0:T(4,128)S(1)}, u32[]{:S(2)}, u32[]{:S(2)}) %collective-permute-start.18) | collective-permute-done | bytes 12320 | tf_op jit(solution)/shard_map/ppermute | solution.py:416
  69.2 4.4 %collective-permute-start.19 = (f32[3,4,256]{2,1,0:T(4,128)S(1)}, f32[3,4,256]{2,1,0:T(4,128)S(1)}, u32[]{:S(2)}, u32[]{:S(2)}) collective-permute-start(f32[3,4,256]{2,1,0:T(4,128)S(1)} %add.51), channel_id=1, source_target_pairs={{0,128},{4,132},{8,136},{12,140},{16,144},{20,148},{24,152},{28,15... | collective-permute-start | bytes 36872 | tf_op jit(solution)/shard_map/ppermute | solution.py:423
  73.6 2.4 %collective-permute-start.20 = (f32[3,4,256]{2,1,0:T(4,128)S(1)}, f32[3,4,256]{2,1,0:T(4,128)S(1)}, u32[]{:S(2)}, u32[]{:S(2)}) collective-permute-start(f32[3,4,256]{2,1,0:T(4,128)S(1)} %add.51), channel_id=1, source_target_pairs={{0,64},{4,68},{8,72},{12,76},{16,80},{20,84},{24,88},{28,92},{32,9... | collective-permute-start | bytes 36872 | tf_op jit(solution)/shard_map/ppermute | solution.py:423
  76.0 1.8 %collective-permute-start.21 = (f32[3,4,256]{2,1,0:T(4,128)S(1)}, f32[3,4,256]{2,1,0:T(4,128)S(1)}, u32[]{:S(2)}, u32[]{:S(2)}) collective-permute-start(f32[3,4,256]{2,1,0:T(4,128)S(1)} %add.51), channel_id=1, source_target_pairs={{0,192},{4,196},{8,200},{12,204},{16,208},{20,212},{24,216},{28,22... | collective-permute-start | bytes 36872 | tf_op jit(solution)/shard_map/ppermute | solution.py:423
  77.7 2.6 %shard_map.85 = (f32[48,2048]{1,0:T(8,128)S(1)}, bf16[48,2048]{1,0:T(8,128)(2,1)S(1)}, bf16[48,2048]{1,0:T(8,128)(2,1)S(1)}, bf16[48,2048]{1,0:T(8,128)(2,1)S(1)}) custom-call(s32[4]{0:T(128)S(1)} %pad_add_fusion.me_ref, bf16[3,192,256]{2,1,0:T(8,128)(2,1)S(1)} %get-tuple-element.58.grad_ref, f32[3,16,256]{2,1,0:T(8,128)S(1)} %get-tuple-element.59.tail_ref, ...), custom_call_target="tpu_custom_call" | custom-call | flops 603979776 | bytes 4000000 | tf_op jit(solution)/shard_map/pallas_call | solution.py:490
  80.3 1.7 %collective-permute-start.11 = (bf16[48,2048]{1,0:T(8,128)(2,1)S(1)}, bf16[48,2048]{1,0:T(8,128)(2,1)S(1)}, u32[]{:S(2)}, u32[]{:S(2)}) collective-permute-start(bf16[48,2048]{1,0:T(8,128)(2,1)S(1)} %get-tuple-element.62), channel_id=1, source_target_pairs={{0,1},{1,2},{2,3},{3,0},{4,5},{5,6},{6,7},{7,4},{8,9},{9,10},{10,1... | collective-permute-start | bytes 589832 | tf_op jit(solution)/shard_map/ppermute | solution.py:510
  82.0 2.9 %collective-permute-start.12 = (bf16[48,2048]{1,0:T(8,128)(2,1)S(1)}, bf16[48,2048]{1,0:T(8,128)(2,1)S(1)}, u32[]{:S(2)}, u32[]{:S(2)}) collective-permute-start(bf16[48,2048]{1,0:T(8,128)(2,1)S(1)} %get-tuple-element.63), channel_id=1, source_target_pairs={{0,2},{1,3},{2,0},{3,1},{4,6},{5,7},{6,4},{7,5},{8,10},{9,11},{10,... | collective-permute-start | bytes 589832 | tf_op jit(solution)/shard_map/ppermute | solution.py:510
  84.9 1.3 %collective-permute-start.13 = (bf16[48,2048]{1,0:T(8,128)(2,1)S(1)}, bf16[48,2048]{1,0:T(8,128)(2,1)S(1)}, u32[]{:S(2)}, u32[]{:S(2)}) collective-permute-start(bf16[48,2048]{1,0:T(8,128)(2,1)S(1)} %get-tuple-element.64), channel_id=1, source_target_pairs={{0,3},{1,0},{2,1},{3,2},{4,7},{5,4},{6,5},{7,6},{8,11},{9,8},{10,9... | collective-permute-start | bytes 589832 | tf_op jit(solution)/shard_map/ppermute | solution.py:510
  86.8 2.0 %collective-permute-done.11 = bf16[48,2048]{1,0:T(8,128)(2,1)S(1)} collective-permute-done((bf16[48,2048]{1,0:T(8,128)(2,1)S(1)}, bf16[48,2048]{1,0:T(8,128)(2,1)S(1)}, u32[]{:S(2)}, u32[]{:S(2)}) %collective-permute-start.11) | collective-permute-done | bytes 196640 | tf_op jit(solution)/shard_map/ppermute | solution.py:510
  88.8 3.5 %collective-permute-done.12 = bf16[48,2048]{1,0:T(8,128)(2,1)S(1)} collective-permute-done((bf16[48,2048]{1,0:T(8,128)(2,1)S(1)}, bf16[48,2048]{1,0:T(8,128)(2,1)S(1)}, u32[]{:S(2)}, u32[]{:S(2)}) %collective-permute-start.12) | collective-permute-done | bytes 196640 | tf_op jit(solution)/shard_map/ppermute | solution.py:510
  (41 shorter events, 8.0 us)
Async XLA Ops:
  0.6 1.9 %copy-start = (bf16[3,2048,256]{2,1,0:T(8,128)(2,1)S(1)}, bf16[3,2048,256]{2,1,0:T(8,128)(2,1)}, u32[]{:S(2)}) copy-start(bf16[3,2048,256]{2,1,0:T(8,128)(2,1)} %w_ref.3) | copy-start | bytes 9437188
  2.5 1.1 %copy-start.2 = (bf16[192,2048]{1,0:T(8,128)(2,1)S(1)}, bf16[192,2048]{1,0:T(8,128)(2,1)}, u32[]{:S(2)}) copy-start(bf16[192,2048]{1,0:T(8,128)(2,1)} %x_ref.1) | copy-start | bytes 2359300
  3.7 6.4 %copy-start.3 = (bf16[192,256]{1,0:T(8,128)(2,1)S(1)}, bf16[192,256]{1,0:T(8,128)(2,1)}, u32[]{:S(2)}) copy-start(bf16[192,256]{1,0:T(8,128)(2,1)} %grad_ref.5) | copy-start | bytes 294916
  3.7 6.4 %copy-start.4 = (f32[3,4,256]{2,1,0:T(4,128)S(1)}, f32[3,4,256]{2,1,0:T(4,128)}, u32[]{:S(2)}) copy-start(f32[3,4,256]{2,1,0:T(4,128)} %cw_ref.3) | copy-start | bytes 36868
  3.7 6.4 %copy-start.5 = (s32[2,192]{1,0:T(2,128)S(1)}, s32[2,192]{1,0:T(2,128)}, u32[]{:S(2)}) copy-start(s32[2,192]{1,0:T(2,128)} %gate_ref.1) | copy-start | bytes 4612
  3.7 6.4 %copy-start.6 = (s32[2,192]{1,0:T(2,128)S(1)}, s32[2,192]{1,0:T(2,128)}, u32[]{:S(2)}) copy-start(s32[2,192]{1,0:T(2,128)} %beta_ref.1) | copy-start | bytes 4612
  4.9 5.1 %collective-permute-start = (f32[3,8,256]{2,1,0:T(8,128)S(1)}, f32[3,8,256]{2,1,0:T(8,128)S(1)}, u32[]{:S(2)}, u32[]{:S(2)}) collective-permute-start(f32[3,8,256]{2,1,0:T(8,128)S(1)} %get-tuple-element.35), channel_id=1, source_target_pairs={{0,4},{4,8},{8,12},{12,16},{16,20},{20,24},{24,28},{28,32},{32,36}... | collective-permute-start | bytes 73736 | tf_op jit(solution)/shard_map/ppermute | solution.py:440
  15.6 1.5 %collective-permute-start.1 = (f32[3,128,128]{2,1,0:T(8,128)S(1)}, f32[3,128,128]{2,1,0:T(8,128)S(1)}, u32[]{:S(2)}, u32[]{:S(2)}) collective-permute-start(f32[3,128,128]{2,1,0:T(8,128)S(1)} %get-tuple-element.37), channel_id=1, source_target_pairs={{0,4},{4,0},{8,12},{12,8},{16,20},{20,16},{24,28},{28,24},{32,36},... | collective-permute-start | bytes 589832 | tf_op jit(solution)/shard_map/ppermute | solution.py:416
  18.0 4.9 %collective-permute-start.2 = (bf16[3,128,128]{2,1,0:T(8,128)(2,1)S(1)}, bf16[3,128,128]{2,1,0:T(8,128)(2,1)S(1)}, u32[]{:S(2)}, u32[]{:S(2)}) collective-permute-start(bf16[3,128,128]{2,1,0:T(8,128)(2,1)S(1)} %shard_map.79.own_ref), channel_id=1, source_target_pairs={{0,8},{4,12},{8,16},{12,20},{16,24},{20,28},{24,0},{28,4},{32,40},... | collective-permute-start | bytes 294920 | tf_op jit(solution)/shard_map/ppermute | solution.py:423
  19.5 7.2 %collective-permute-start.3 = (bf16[3,128,128]{2,1,0:T(8,128)(2,1)S(1)}, bf16[3,128,128]{2,1,0:T(8,128)(2,1)S(1)}, u32[]{:S(2)}, u32[]{:S(2)}) collective-permute-start(bf16[3,128,128]{2,1,0:T(8,128)(2,1)S(1)} %shard_map.79.own_ref), channel_id=1, source_target_pairs={{0,16},{4,20},{8,24},{12,28},{16,0},{20,4},{24,8},{28,12},{32,48},... | collective-permute-start | bytes 294920 | tf_op jit(solution)/shard_map/ppermute | solution.py:423
  20.3 6.7 %collective-permute-start.4 = (bf16[3,128,128]{2,1,0:T(8,128)(2,1)S(1)}, bf16[3,128,128]{2,1,0:T(8,128)(2,1)S(1)}, u32[]{:S(2)}, u32[]{:S(2)}) collective-permute-start(bf16[3,128,128]{2,1,0:T(8,128)(2,1)S(1)} %shard_map.79.own_ref), channel_id=1, source_target_pairs={{0,24},{4,28},{8,0},{12,4},{16,8},{20,12},{24,16},{28,20},{32,56},... | collective-permute-start | bytes 294920 | tf_op jit(solution)/shard_map/ppermute | solution.py:423
  28.3 5.6 %collective-permute-start.5 = (bf16[3,128,128]{2,1,0:T(8,128)(2,1)S(1)}, bf16[3,128,128]{2,1,0:T(8,128)(2,1)S(1)}, u32[]{:S(2)}, u32[]{:S(2)}) collective-permute-start(bf16[3,128,128]{2,1,0:T(8,128)(2,1)S(1)} %get-tuple-element.38.own_ref), channel_id=1, source_target_pairs={{0,32},{4,36},{8,40},{12,44},{16,48},{20,52},{24,56},{28,60},{32,0... | collective-permute-start | bytes 294920 | tf_op jit(solution)/shard_map/ppermute | solution.py:416
  34.6 12.6 %collective-permute-start.6 = (bf16[2,128,128]{2,1,0:T(8,128)(2,1)S(1)}, bf16[2,128,128]{2,1,0:T(8,128)(2,1)S(1)}, u32[]{:S(2)}, u32[]{:S(2)}) collective-permute-start(bf16[2,128,128]{2,1,0:T(8,128)(2,1)S(1)} %get-tuple-element.39), channel_id=1, source_target_pairs={{0,64},{4,68},{8,72},{12,76},{16,80},{20,84},{24,88},{28,92},{32,9... | collective-permute-start | bytes 196616 | tf_op jit(solution)/shard_map/ppermute | solution.py:423
  38.1 9.1 %collective-permute-start.7 = (bf16[2,128,128]{2,1,0:T(8,128)(2,1)S(1)}, bf16[2,128,128]{2,1,0:T(8,128)(2,1)S(1)}, u32[]{:S(2)}, u32[]{:S(2)}) collective-permute-start(bf16[2,128,128]{2,1,0:T(8,128)(2,1)S(1)} %get-tuple-element.40), channel_id=1, source_target_pairs={{0,128},{4,132},{8,136},{12,140},{16,144},{20,148},{24,152},{28,15... | collective-permute-start | bytes 196616 | tf_op jit(solution)/shard_map/ppermute | solution.py:423
  43.5 6.0 %collective-permute-start.8 = (bf16[2,128,128]{2,1,0:T(8,128)(2,1)S(1)}, bf16[2,128,128]{2,1,0:T(8,128)(2,1)S(1)}, u32[]{:S(2)}, u32[]{:S(2)}) collective-permute-start(bf16[2,128,128]{2,1,0:T(8,128)(2,1)S(1)} %get-tuple-element.41), channel_id=1, source_target_pairs={{0,192},{4,196},{8,200},{12,204},{16,208},{20,212},{24,216},{28,22... | collective-permute-start | bytes 196616 | tf_op jit(solution)/shard_map/ppermute | solution.py:423
  50.9 2.7 %collective-permute-start.9 = (f32[2,128,128]{2,1,0:T(8,128)S(1)}, f32[2,128,128]{2,1,0:T(8,128)S(1)}, u32[]{:S(2)}, u32[]{:S(2)}) collective-permute-start(f32[2,128,128]{2,1,0:T(8,128)S(1)} %get-tuple-element.45), channel_id=1, source_target_pairs={{0,4},{4,0},{8,12},{12,8},{16,20},{20,16},{24,28},{28,24},{32,36},... | collective-permute-start | bytes 393224 | tf_op jit(solution)/shard_map/ppermute | solution.py:416
  53.6 24.2 %copy-start.1 = (bf16[3,2048,256]{2,1,0:T(8,128)(2,1)S(1)}, bf16[3,2048,256]{2,1,0:T(8,128)(2,1)}, u32[]{:S(2)}) copy-start(bf16[3,2048,256]{2,1,0:T(8,128)(2,1)} %w_ref.3) | copy-start | bytes 9437188
  56.9 1.4 %collective-permute-start.14 = (f32[3,4,256]{2,1,0:T(4,128)S(1)}, f32[3,4,256]{2,1,0:T(4,128)S(1)}, u32[]{:S(2)}, u32[]{:S(2)}) collective-permute-start(f32[3,4,256]{2,1,0:T(4,128)S(1)} %get-tuple-element.65), channel_id=1, source_target_pairs={{0,4},{4,0},{8,12},{12,8},{16,20},{20,16},{24,28},{28,24},{32,36},... | collective-permute-start | bytes 36872 | tf_op jit(solution)/shard_map/ppermute | solution.py:416
  58.4 6.8 %collective-permute-start.15 = (f32[3,4,256]{2,1,0:T(4,128)S(1)}, f32[3,4,256]{2,1,0:T(4,128)S(1)}, u32[]{:S(2)}, u32[]{:S(2)}) collective-permute-start(f32[3,4,256]{2,1,0:T(4,128)S(1)} %add.47), channel_id=1, source_target_pairs={{0,16},{4,20},{8,24},{12,28},{16,0},{20,4},{24,8},{28,12},{32,48},... | collective-permute-start | bytes 36872 | tf_op jit(solution)/shard_map/ppermute | solution.py:423
  61.3 4.0 %collective-permute-start.16 = (f32[3,4,256]{2,1,0:T(4,128)S(1)}, f32[3,4,256]{2,1,0:T(4,128)S(1)}, u32[]{:S(2)}, u32[]{:S(2)}) collective-permute-start(f32[3,4,256]{2,1,0:T(4,128)S(1)} %add.47), channel_id=1, source_target_pairs={{0,8},{4,12},{8,16},{12,20},{16,24},{20,28},{24,0},{28,4},{32,40},... | collective-permute-start | bytes 36872 | tf_op jit(solution)/shard_map/ppermute | solution.py:423
  61.7 3.7 %collective-permute-start.17 = (f32[3,4,256]{2,1,0:T(4,128)S(1)}, f32[3,4,256]{2,1,0:T(4,128)S(1)}, u32[]{:S(2)}, u32[]{:S(2)}) collective-permute-start(f32[3,4,256]{2,1,0:T(4,128)S(1)} %add.47), channel_id=1, source_target_pairs={{0,24},{4,28},{8,0},{12,4},{16,8},{20,12},{24,16},{28,20},{32,56},... | collective-permute-start | bytes 36872 | tf_op jit(solution)/shard_map/ppermute | solution.py:423
  63.3 14.4 %collective-permute-start.10 = (f32[3,8,256]{2,1,0:T(8,128)S(1)}, f32[3,8,256]{2,1,0:T(8,128)S(1)}, u32[]{:S(2)}, u32[]{:S(2)}) collective-permute-start(f32[3,8,256]{2,1,0:T(8,128)S(1)} %get-tuple-element.60), channel_id=1, source_target_pairs={{4,0},{8,4},{12,8},{16,12},{20,16},{24,20},{28,24},{32,28},{36,32}... | collective-permute-start | bytes 73736 | tf_op jit(solution)/shard_map/ppermute | solution.py:486
  65.4 3.8 %collective-permute-start.18 = (f32[3,4,256]{2,1,0:T(4,128)S(1)}, f32[3,4,256]{2,1,0:T(4,128)S(1)}, u32[]{:S(2)}, u32[]{:S(2)}) collective-permute-start(f32[3,4,256]{2,1,0:T(4,128)S(1)} %add_add_fusion.1), channel_id=1, source_target_pairs={{0,32},{4,36},{8,40},{12,44},{16,48},{20,52},{24,56},{28,60},{32,0... | collective-permute-start | bytes 36872 | tf_op jit(solution)/shard_map/ppermute | solution.py:416
  69.2 15.7 %collective-permute-start.19 = (f32[3,4,256]{2,1,0:T(4,128)S(1)}, f32[3,4,256]{2,1,0:T(4,128)S(1)}, u32[]{:S(2)}, u32[]{:S(2)}) collective-permute-start(f32[3,4,256]{2,1,0:T(4,128)S(1)} %add.51), channel_id=1, source_target_pairs={{0,128},{4,132},{8,136},{12,140},{16,144},{20,148},{24,152},{28,15... | collective-permute-start | bytes 36872 | tf_op jit(solution)/shard_map/ppermute | solution.py:423
  73.6 12.6 %collective-permute-start.20 = (f32[3,4,256]{2,1,0:T(4,128)S(1)}, f32[3,4,256]{2,1,0:T(4,128)S(1)}, u32[]{:S(2)}, u32[]{:S(2)}) collective-permute-start(f32[3,4,256]{2,1,0:T(4,128)S(1)} %add.51), channel_id=1, source_target_pairs={{0,64},{4,68},{8,72},{12,76},{16,80},{20,84},{24,88},{28,92},{32,9... | collective-permute-start | bytes 36872 | tf_op jit(solution)/shard_map/ppermute | solution.py:423
  76.0 10.3 %collective-permute-start.21 = (f32[3,4,256]{2,1,0:T(4,128)S(1)}, f32[3,4,256]{2,1,0:T(4,128)S(1)}, u32[]{:S(2)}, u32[]{:S(2)}) collective-permute-start(f32[3,4,256]{2,1,0:T(4,128)S(1)} %add.51), channel_id=1, source_target_pairs={{0,192},{4,196},{8,200},{12,204},{16,208},{20,212},{24,216},{28,22... | collective-permute-start | bytes 36872 | tf_op jit(solution)/shard_map/ppermute | solution.py:423
  80.3 8.5 %collective-permute-start.11 = (bf16[48,2048]{1,0:T(8,128)(2,1)S(1)}, bf16[48,2048]{1,0:T(8,128)(2,1)S(1)}, u32[]{:S(2)}, u32[]{:S(2)}) collective-permute-start(bf16[48,2048]{1,0:T(8,128)(2,1)S(1)} %get-tuple-element.62), channel_id=1, source_target_pairs={{0,1},{1,2},{2,3},{3,0},{4,5},{5,6},{6,7},{7,4},{8,9},{9,10},{10,1... | collective-permute-start | bytes 589832 | tf_op jit(solution)/shard_map/ppermute | solution.py:510
  82.0 10.4 %collective-permute-start.12 = (bf16[48,2048]{1,0:T(8,128)(2,1)S(1)}, bf16[48,2048]{1,0:T(8,128)(2,1)S(1)}, u32[]{:S(2)}, u32[]{:S(2)}) collective-permute-start(bf16[48,2048]{1,0:T(8,128)(2,1)S(1)} %get-tuple-element.63), channel_id=1, source_target_pairs={{0,2},{1,3},{2,0},{3,1},{4,6},{5,7},{6,4},{7,5},{8,10},{9,11},{10,... | collective-permute-start | bytes 589832 | tf_op jit(solution)/shard_map/ppermute | solution.py:510
  84.9 7.5 %collective-permute-start.13 = (bf16[48,2048]{1,0:T(8,128)(2,1)S(1)}, bf16[48,2048]{1,0:T(8,128)(2,1)S(1)}, u32[]{:S(2)}, u32[]{:S(2)}) collective-permute-start(bf16[48,2048]{1,0:T(8,128)(2,1)S(1)} %get-tuple-element.64), channel_id=1, source_target_pairs={{0,3},{1,0},{2,1},{3,2},{4,7},{5,4},{6,5},{7,6},{8,11},{9,8},{10,9... | collective-permute-start | bytes 589832 | tf_op jit(solution)/shard_map/ppermute | solution.py:510
where the time goes:
time: 93.3 us; the launch traced here: 93.1 us
  starting transfers between devices  44.9 us (48%)
  waiting for transfers between devices  23.4 us (25%)
  Pallas kernels  19.4 us (21%)
  local copies, waits for them, and re-layouts  3.04 us (3%)
  other arithmetic  1.48 us (2%)
    ppermute x12, starting transfers between devices, turn(): return lax.ppermute(block, 'ctx', route)  30.8 us
    pallas_call x7, Pallas kernels, run(): pl.pallas_call(kernel, out_shape=out_shape, in_specs=specs, out_specs=jax...  15.6 us
    ppermute x5, waiting for transfers between devices, swap(): return lax.ppermute(block, 'ctx', [(i, i ^ bit) for i in range(n)])  8.22 us
    ppermute x12, waiting for transfers between devices, turn(): return lax.ppermute(block, 'ctx', route)  6.58 us
    ppermute x3, starting transfers between devices, body(): lax.ppermute(block, 'head', [(i, (i + shift) % heads) for i in range(head...  5.91 us
    ppermute x3, waiting for transfers between devices, body(): lax.ppermute(block, 'head', [(i, (i + shift) % heads) for i in range(head...  5.53 us
    ppermute x5, starting transfers between devices, swap(): return lax.ppermute(block, 'ctx', [(i, i ^ bit) for i in range(n)])  4.37 us
    ppermute x1, waiting for transfers between devices, body(): halo = lax.ppermute(tail, 'ctx', [(i, i + 1) for i in range(n - 1)])  3.1 us
  transfers between devices with their start and end apart: 22, of which 12 were waited for; matrix products, arithmetic and copies ran while one was open for 1% of the time, Pallas kernels for 5%

commit v1 on v0

--- a/solution.py
+++ b/solution.py
@@ -14,7 +14,6 @@
 SCALE = DK**-0.5
 F32 = jnp.float32
 BF16 = jnp.bfloat16
-HIGHEST = lax.Precision.HIGHEST
 NN = (((1,), (0,)), ((), ()))
 NT = (((1,), (1,)), ((), ()))
 TN = (((0,), (0,)), ((), ()))
@@ -45,8 +44,9 @@
     return dot(a, bh, dims) + dot(a, bl, dims)
 
 
-def exact(a, b, dims):
-    return lax.dot_general(a, b, dims, precision=HIGHEST, preferred_element_type=F32)
+def pieces(a):
+    high, low = split(a)
+    return high, low, (a - high.astype(F32) - low.astype(F32)).astype(BF16)
 
 
 def iotas(rows, cols):
@@ -87,11 +87,19 @@
     return jax.ShapeDtypeStruct(s, d)
 
 
-def project_kernel(x_ref, w_ref, o_ref, tail_ref):
-    value = dot(x_ref[...], w_ref[0], NN).astype(BF16)
-    o_ref[0] = value
-    rows = value.shape[0]
-    tail_ref[0] = value[rows - 16 :].astype(F32)[8:]
+def project_kernel(x_ref, w_ref, o_ref, tail_ref, x_held, w_held, sems):
+    copies = [pltpu.make_async_copy(x_ref, x_held, sems.at[3])]
+    for m in range(3):
+        copies.append(pltpu.make_async_copy(w_ref.at[m], w_held.at[m], sems.at[m]))
+    for copy in copies:
+        copy.start()
+    copies[0].wait()
+    rows = x_ref.shape[0]
+    for m in range(3):
+        copies[1 + m].wait()
+        value = dot(x_held[...], w_held[m], NN).astype(BF16)
+        o_ref[m] = value
+        tail_ref[m] = value[rows - 16 :].astype(F32)[8:]
 
 
 def sigmoid(z):
@@ -118,11 +126,11 @@
     logs = jnp.log(1.0 - 0.001 * gate_ref[...].astype(F32) / 1023.0)
     beta = beta_ref[...].astype(F32) / 1023.0
     r, c = iotas(rows, rows)
-    tri = (r >= c).astype(F32)
-    col = exact(tri, logs, NT)
-    row = exact(logs, tri, NT)
-    betas = exact((r == c).astype(F32), beta, NT)
-    r64, c64 = iotas(BLOCK, BLOCK)
+    tri = jnp.where(r >= c, 1.0, 0.0).astype(BF16)
+    unit = jnp.where(r == c, 1.0, 0.0).astype(BF16)
+    col = sum(dot(tri, piece, NT) for piece in pieces(logs))
+    row = sum(dot(piece, tri, NT) for piece in pieces(logs))
+    betas = sum(dot(unit, piece, NT) for piece in pieces(beta))
     diag = []
     keys = []
     queries = []
@@ -137,7 +145,8 @@
         decay = jnp.where(r >= c, jnp.exp(b - row[h : h + 1]), 0.0)
         d_ref[h] = decay
         gram = mm(keys[h], keys[h], NT)
-        a_ref[h] = jnp.where(r > c, decay * gram * bt, 0.0)
+        low = jnp.where(r > c, decay * gram * bt, 0.0)
+        a_ref[h] = low
         p_ref[h] = decay * mm(queries[h], keys[h], NT)
         q_ref[h] = queries[h]
         k_ref[h] = keys[h]
@@ -147,10 +156,7 @@
         col_ref[h, 2] = jnp.broadcast_to(jnp.exp(total - b), (rows, DK))
         for i in range(blocks):
             span = slice(i * BLOCK, (i + 1) * BLOCK)
-            kb = keys[h][span]
-            rb = exact(logs, tri[span], NT)[h : h + 1]
-            dec = jnp.exp(b[span] - rb)
-            diag.append(jnp.where(r64 > c64, dec * mm(kb, kb, NT) * bt[span], 0.0))
+            diag.append(low[span, span])
     lower = jnp.stack(diag)
     count = len(diag)
     tiles = []
@@ -374,7 +380,8 @@
             first = tap * dzs[m, 3 - j : 11 - j]
             dx = term if dx is None else dx + term
             spill = first if spill is None else spill + first
-            taps_ref[m, j : j + 1] = jnp.sum(dz * ext[m, 5 + j : 5 + j + rows], 0, keepdims=True)
+            tap = jnp.sum(dz * ext[m, 5 + j : 5 + j + rows], 0, keepdims=True)
+            taps_ref[m, j : j + 1] = tap
         out_ref[m] = dx.astype(BF16)
         tail_ref[m] = dx[rows - 16 :]
         spill_ref[m] = spill
@@ -425,17 +432,15 @@
 
     projected, tail = pl.pallas_call(
         project_kernel,
-        grid=(3,),
-        in_specs=[
-            pl.BlockSpec((rows, width), lambda m: (0, 0)),
-            pl.BlockSpec((1, width, lanes), lambda m: (m, 0, 0)),
+        in_specs=[pl.BlockSpec(memory_space=pl.ANY)] * 2,
+        out_specs=(pl.BlockSpec(memory_space=pltpu.VMEM),) * 2,
+        out_shape=(shape((3, rows, lanes), BF16), shape((3, 8, lanes))),
+        scratch_shapes=[
+            pltpu.VMEM((rows, width), BF16),
+            pltpu.VMEM((3, width, lanes), BF16),
+            pltpu.SemaphoreType.DMA((4,)),
         ],
-        out_specs=(
-            pl.BlockSpec((1, rows, lanes), lambda m: (m, 0, 0)),
-            pl.BlockSpec((1, 8, lanes), lambda m: (m, 0, 0)),
-        ),
-        out_shape=(shape((3, rows, lanes), BF16), shape((3, 8, lanes))),
-        compiler_params=pltpu.CompilerParams(vmem_limit_bytes=LIMIT),
+        compiler_params=pltpu.CompilerParams(vmem_limit_bytes=66_500_000),
     )(inputs, projection)
     halo = lax.ppermute(tail, "ctx", [(i, i + 1) for i in range(n - 1)])
     square = (2, rows, rows)
@@ -509,15 +514,14 @@
     for shift, block in enumerate(sends, 1):
         got = lax.ppermute(block, "head", [(i, (i + shift) % heads) for i in range(heads)])
         total = total + got.astype(F32)
-
-    def around(taps, stride):
-        r1, r2, r3 = (turn(taps, stride, k) for k in (1, 2, 3))
-        return (taps + r2) + (r1 + r3)
-
+    zs = n // (2 * XS)
+    column = [[z * 2 * XS + i for z in range(zs)] for i in range(2 * XS)]
     taps = taps + swap(taps, 1)
-    taps = around(taps, 2)
-    taps = taps + swap(taps, 2 * XS)
-    taps = around(taps, 4 * XS)
+    r1, r2, r3 = (turn(taps, 2, k) for k in (1, 2, 3))
+    taps = (taps + r2) + (r1 + r3)
+    taps = jnp.broadcast_to(taps, (zs,) + taps.shape)
+    taps = lax.all_to_all(taps, "ctx", 0, 0, axis_index_groups=column)
+    taps = jnp.sum(taps, 0)
     return (total.astype(BF16), taps)
 
 

time: 93.3 us -> 90.9 us (0.974)
  the two profiles are of different devices: /device:TPU:2 before, /device:TPU:4 now
where the time goes in v1:
time: 90.9 us; the launch traced here: 90.7 us
  starting transfers between devices  33.1 us (36%)
  Pallas kernels  21.4 us (24%)
  waiting for transfers between devices  16.9 us (19%)
  blocking collectives  15.9 us (17%)
  other arithmetic  1.48 us (2%)
  local copies, waits for them, and re-layouts  1 us (1%)
    ppermute x9, starting transfers between devices, turn(): return lax.ppermute(block, 'ctx', route)  19.3 us
    all_to_all x1, blocking collectives, body(): taps = lax.all_to_all(taps, 'ctx', 0, 0, axis_index_groups=column)  15.9 us
    pallas_call x7, Pallas kernels, run(): pl.pallas_call(kernel, out_shape=out_shape, in_specs=specs, out_specs=jax...  15 us
    ppermute x9, waiting for transfers between devices, turn(): return lax.ppermute(block, 'ctx', route)  8.29 us
    ppermute x3, starting transfers between devices, body(): lax.ppermute(block, 'head', [(i, (i + shift) % heads) for i in range(head...  5.91 us
    ppermute x4, waiting for transfers between devices, swap(): return lax.ppermute(block, 'ctx', [(i, i ^ bit) for i in range(n)])  5.34 us
    pallas_call x1, Pallas kernels, body(): pl.pallas_call(project_kernel, in_specs=[pl.BlockSpec(memory_space=pl.ANY...  3.75 us
    ppermute x1, starting transfers between devices, body(): spill = lax.ppermute(spill, 'ctx', [(i + 1, i) for i in range(n - 1)])  3.56 us
  transfers between devices with their start and end apart: 18, of which 8 were waited for; matrix products, arithmetic and copies ran while one was open for 1% of the time, Pallas kernels for 5%

profile of v1, /device:TPU:4, one launch (start us, length us, event | category | flops | bytes accessed | tf_op | source)
XLA Modules:
  0.0 90.7 jit_solution(2815449556615217834)
XLA Ops:
  0.7 3.7 %shard_map.77 = (bf16[3,192,256]{2,1,0:T(8,128)(2,1)}, f32[3,8,256]{2,1,0:T(8,128)}) custom-call(bf16[192,2048]{1,0:T(8,128)(2,1)} %x_ref.1, bf16[3,2048,256]{2,1,0:T(8,128)(2,1)} %w_ref.3), custom_call_target="tpu_custom_call" | custom-call | tf_op jit(solution)/shard_map/pallas_call | solution.py:433
  4.4 1.9 %collective-permute-start = (f32[3,8,256]{2,1,0:T(8,128)}, f32[3,8,256]{2,1,0:T(8,128)S(1)}, u32[]{:S(2)}, u32[]{:S(2)}) collective-permute-start(f32[3,8,256]{2,1,0:T(8,128)} %get-tuple-element.35), channel_id=1, source_target_pairs={{0,4},{4,8},{8,12},{12,16},{16,20},{20,24},{24,28},{28,32},{32,36}... | collective-permute-start | bytes 73736 | tf_op jit(solution)/shard_map/ppermute | solution.py:445
  6.5 3.3 %collective-permute-done.halo_ref = f32[3,8,256]{2,1,0:T(8,128)S(1)} collective-permute-done((f32[3,8,256]{2,1,0:T(8,128)}, f32[3,8,256]{2,1,0:T(8,128)S(1)}, u32[]{:S(2)}, u32[]{:S(2)}) %collective-permute-start) | collective-permute-done | bytes 24608 | tf_op jit(solution)/shard_map/ppermute | solution.py:445
  9.8 1.0 %copy-done.2 = bf16[3,192,256]{2,1,0:T(8,128)(2,1)S(1)} copy-done((bf16[3,192,256]{2,1,0:T(8,128)(2,1)S(1)}, bf16[3,192,256]{2,1,0:T(8,128)(2,1)}, u32[]{:S(2)}) %copy-start.2) | copy-done | bytes 294936
  10.8 5.0 %shard_map.78 = (f32[3,128,128]{2,1,0:T(8,128)S(1)}, f32[3,128,128]{2,1,0:T(8,128)S(1)}, f32[3,192,256]{2,1,0:T(8,128)S(1)}, f32[2,192,128]{2,1,0:T(8,128)S(1)},...) custom-call(s32[4]{0:T(128)S(1)} %pad_add_fusion.me_ref, ...), custom_call_target="tpu_custom_call" | custom-call | flops 2000000000 | bytes 4000000 | tf_op jit(solution)/shard_map/pallas_call | solution.py:70
  15.9 1.4 %collective-permute-done.1.recv_ref = f32[3,128,128]{2,1,0:T(8,128)S(1)} collective-permute-done((f32[3,128,128]{2,1,0:T(8,128)S(1)}, f32[3,128,128]{2,1,0:T(8,128)S(1)}, u32[]{:S(2)}, u32[]{:S(2)}) %collective-permute-start.1) | collective-permute-done | bytes 196640 | tf_op jit(solution)/shard_map/ppermute | solution.py:423
  17.3 0.8 shard_map.79.own_ref
  18.1 1.3 %collective-permute-start.2 = (bf16[3,128,128]{2,1,0:T(8,128)(2,1)S(1)}, bf16[3,128,128]{2,1,0:T(8,128)(2,1)S(1)}, u32[]{:S(2)}, u32[]{:S(2)}) collective-permute-start(bf16[3,128,128]{2,1,0:T(8,128)(2,1)S(1)} %shard_map.79.own_ref), channel_id=1, source_target_pairs={{0,8},{4,12},{8,16},{12,20},{16,24},{20,28},{24,0},{28,4},{32,40},... | collective-permute-start | bytes 294920 | tf_op jit(solution)/shard_map/ppermute | solution.py:430
  19.4 0.8 collective-permute-start.3
  20.9 2.1 %collective-permute-done.2.r1 = bf16[3,128,128]{2,1,0:T(8,128)(2,1)S(1)} collective-permute-done((bf16[3,128,128]{2,1,0:T(8,128)(2,1)S(1)}, bf16[3,128,128]{2,1,0:T(8,128)(2,1)S(1)}, u32[]{:S(2)}, u32[]{:S(2)}) %collective-permute-start.2) | collective-permute-done | bytes 98336 | tf_op jit(solution)/shard_map/ppermute | solution.py:430
  23.0 2.5 %collective-permute-done.3.r2 = bf16[3,128,128]{2,1,0:T(8,128)(2,1)S(1)} collective-permute-done((bf16[3,128,128]{2,1,0:T(8,128)(2,1)S(1)}, bf16[3,128,128]{2,1,0:T(8,128)(2,1)S(1)}, u32[]{:S(2)}, u32[]{:S(2)}) %collective-permute-start.3) | collective-permute-done | bytes 98336 | tf_op jit(solution)/shard_map/ppermute | solution.py:430
  25.5 1.5 %collective-permute-done.4.r3 = bf16[3,128,128]{2,1,0:T(8,128)(2,1)S(1)} collective-permute-done((bf16[3,128,128]{2,1,0:T(8,128)(2,1)S(1)}, bf16[3,128,128]{2,1,0:T(8,128)(2,1)S(1)}, u32[]{:S(2)}, u32[]{:S(2)}) %collective-permute-start.4) | collective-permute-done | bytes 98336 | tf_op jit(solution)/shard_map/ppermute | solution.py:430
  27.0 1.4 %shard_map.80 = (f32[2,128,128]{2,1,0:T(8,128)S(1)}, f32[2,128,128]{2,1,0:T(8,128)S(1)}, bf16[3,128,128]{2,1,0:T(8,128)(2,1)S(1)}) custom-call(s32[4]{0:T(128)S(1)} %pad_add_fusion.me_ref, bf16[3,128,128]{2,1,0:T(8,128)(2,1)S(1)} %shard_map.79.own_ref, bf16[3,128,128]{2,1,0:T(8,128)(2,1)S(1)} %collective-permute-done.2.r1, ...), custom_call_target="tpu_custom_call" | custom-call | bytes 4000000 | tf_op jit(solution)/shard_map/pallas_call | solution.py:70
  28.3 2.0 %collective-permute-start.5 = (bf16[3,128,128]{2,1,0:T(8,128)(2,1)S(1)}, bf16[3,128,128]{2,1,0:T(8,128)(2,1)S(1)}, u32[]{:S(2)}, u32[]{:S(2)}) collective-permute-start(bf16[3,128,128]{2,1,0:T(8,128)(2,1)S(1)} %get-tuple-element.38.own_ref), channel_id=1, source_target_pairs={{0,32},{4,36},{8,40},{12,44},{16,48},{20,52},{24,56},{28,60},{32,0... | collective-permute-start | bytes 294920 | tf_op jit(solution)/shard_map/ppermute | solution.py:423
  30.3 2.7 %collective-permute-done.5.recv_ref.near_ref = bf16[3,128,128]{2,1,0:T(8,128)(2,1)S(1)} collective-permute-done((bf16[3,128,128]{2,1,0:T(8,128)(2,1)S(1)}, bf16[3,128,128]{2,1,0:T(8,128)(2,1)S(1)}, u32[]{:S(2)}, u32[]{:S(2)}) %collective-permute-start.5) | collective-permute-done | bytes 98336 | tf_op jit(solution)/shard_map/ppermute | solution.py:423
  33.8 3.3 %collective-permute-start.6 = (bf16[2,128,128]{2,1,0:T(8,128)(2,1)S(1)}, bf16[2,128,128]{2,1,0:T(8,128)(2,1)S(1)}, u32[]{:S(2)}, u32[]{:S(2)}) collective-permute-start(bf16[2,128,128]{2,1,0:T(8,128)(2,1)S(1)} %get-tuple-element.39), channel_id=1, source_target_pairs={{0,64},{4,68},{8,72},{12,76},{16,80},{20,84},{24,88},{28,92},{32,9... | collective-permute-start | bytes 196616 | tf_op jit(solution)/shard_map/ppermute | solution.py:430
  37.1 5.4 %collective-permute-start.7 = (bf16[2,128,128]{2,1,0:T(8,128)(2,1)S(1)}, bf16[2,128,128]{2,1,0:T(8,128)(2,1)S(1)}, u32[]{:S(2)}, u32[]{:S(2)}) collective-permute-start(bf16[2,128,128]{2,1,0:T(8,128)(2,1)S(1)} %get-tuple-element.40), channel_id=1, source_target_pairs={{0,128},{4,132},{8,136},{12,140},{16,144},{20,148},{24,152},{28,15... | collective-permute-start | bytes 196616 | tf_op jit(solution)/shard_map/ppermute | solution.py:430
  42.5 3.9 %collective-permute-start.8 = (bf16[2,128,128]{2,1,0:T(8,128)(2,1)S(1)}, bf16[2,128,128]{2,1,0:T(8,128)(2,1)S(1)}, u32[]{:S(2)}, u32[]{:S(2)}) collective-permute-start(bf16[2,128,128]{2,1,0:T(8,128)(2,1)S(1)} %get-tuple-element.41), channel_id=1, source_target_pairs={{0,192},{4,196},{8,200},{12,204},{16,208},{20,212},{24,216},{28,22... | collective-permute-start | bytes 196616 | tf_op jit(solution)/shard_map/ppermute | solution.py:430
  46.3 2.3 %collective-permute-done.8.r3 = bf16[2,128,128]{2,1,0:T(8,128)(2,1)S(1)} collective-permute-done((bf16[2,128,128]{2,1,0:T(8,128)(2,1)S(1)}, bf16[2,128,128]{2,1,0:T(8,128)(2,1)S(1)}, u32[]{:S(2)}, u32[]{:S(2)}) %collective-permute-start.8) | collective-permute-done | bytes 65568 | tf_op jit(solution)/shard_map/ppermute | solution.py:430
  48.6 1.4 %shard_map.82 = (f32[2,128,128]{2,1,0:T(8,128)S(1)}, f32[2,128,128]{2,1,0:T(8,128)S(1)}) custom-call(s32[4]{0:T(128)S(1)} %pad_add_fusion.me_ref, bf16[2,128,128]{2,1,0:T(8,128)(2,1)S(1)} %collective-permute-done.6.r1, bf16[2,128,128]{2,1,0:T(8,128)(2,1)S(1)} %collective-permute-done.7.r2, bf16[2,128,128]{2,1,0:T(8,128)(2,1)S(1)} %collective-permute-done.8.r3, ...), custom_call_target="tpu_custom_call" | custom-call | bytes 4000000 | tf_op jit(solution)/shard_map/pallas_call | solution.py:70
  50.3 2.4 %shard_map.83 = (f32[2,192,128]{2,1,0:T(8,128)S(1)}, f32[2,192,128]{2,1,0:T(8,128)S(1)}) custom-call(f32[2,192,192]{2,1,0:T(8,128)S(1)} %get-tuple-element.53.p_ref, f32[2,192,192]{2,1,0:T(8,128)S(1)} %get-tuple-element.54.a_ref, f32[2,3,64,64]{3,2,1,0:T(8,128)S(1)} %get-tuple-element.55.t_ref, f32[2,192,128]{2,1,0:T(8,128)S(1)} %get-tuple-element.48.k_ref, ...), custom_call_target="tpu_custom_call" | custom-call | flops 500000000 | bytes 4000000 | tf_op jit(solution)/shard_map/pallas_call | solution.py:70
  52.7 3.4 %shard_map.84 = (bf16[3,192,256]{2,1,0:T(8,128)(2,1)S(1)}, f32[3,16,256]{2,1,0:T(8,128)S(1)}, f32[3,8,256]{2,1,0:T(8,128)S(1)}, f32[3,4,256]{2,1,0:T(4,128)S(1)}) custom-call(s32[4]{0:T(128)S(1)} %pad_add_fusion.me_ref, f32[2,128,128]{2,1,0:T(8,128)S(1)} %get-tuple-element.44.own_ref, f32[2,128,128]{2,1,0:T(8,128)S(1)} %collective-permute-done.9.recv_ref, ...), custom_call_target="tpu_custom_call" | custom-call | flops 2000000000 | bytes 4000000 | tf_op jit(solution)/shard_map/pallas_call | solution.py:70
  56.1 3.6 %collective-permute-start.10 = (f32[3,8,256]{2,1,0:T(8,128)S(1)}, f32[3,8,256]{2,1,0:T(8,128)S(1)}, u32[]{:S(2)}, u32[]{:S(2)}) collective-permute-start(f32[3,8,256]{2,1,0:T(8,128)S(1)} %get-tuple-element.60), channel_id=1, source_target_pairs={{4,0},{8,4},{12,8},{16,12},{20,16},{24,20},{28,24},{32,28},{36,32}... | collective-permute-start | bytes 73736 | tf_op jit(solution)/shard_map/ppermute | solution.py:491
  59.7 1.2 %collective-permute-done.14 = f32[3,4,256]{2,1,0:T(4,128)S(1)} collective-permute-done((f32[3,4,256]{2,1,0:T(4,128)S(1)}, f32[3,4,256]{2,1,0:T(4,128)S(1)}, u32[]{:S(2)}, u32[]{:S(2)}) %collective-permute-start.14) | collective-permute-done | bytes 12320 | tf_op jit(solution)/shard_map/ppermute | solution.py:423
  60.9 1.4 %collective-permute-start.15 = (f32[3,4,256]{2,1,0:T(4,128)S(1)}, f32[3,4,256]{2,1,0:T(4,128)S(1)}, u32[]{:S(2)}, u32[]{:S(2)}) collective-permute-start(f32[3,4,256]{2,1,0:T(4,128)S(1)} %add.35), channel_id=1, source_target_pairs={{0,16},{4,20},{8,24},{12,28},{16,0},{20,4},{24,8},{28,12},{32,48},... | collective-permute-start | bytes 36872 | tf_op jit(solution)/shard_map/ppermute | solution.py:430
  62.3 2.6 %collective-permute-start.16 = (f32[3,4,256]{2,1,0:T(4,128)S(1)}, f32[3,4,256]{2,1,0:T(4,128)S(1)}, u32[]{:S(2)}, u32[]{:S(2)}) collective-permute-start(f32[3,4,256]{2,1,0:T(4,128)S(1)} %add.35), channel_id=1, source_target_pairs={{0,8},{4,12},{8,16},{12,20},{16,24},{20,28},{24,0},{28,4},{32,40},... | collective-permute-start | bytes 36872 | tf_op jit(solution)/shard_map/ppermute | solution.py:430
  64.8 2.6 %shard_map.85 = (f32[48,2048]{1,0:T(8,128)S(1)}, bf16[48,2048]{1,0:T(8,128)(2,1)S(1)}, bf16[48,2048]{1,0:T(8,128)(2,1)S(1)}, bf16[48,2048]{1,0:T(8,128)(2,1)S(1)}) custom-call(s32[4]{0:T(128)S(1)} %pad_add_fusion.me_ref, bf16[3,192,256]{2,1,0:T(8,128)(2,1)S(1)} %get-tuple-element.58.grad_ref, f32[3,16,256]{2,1,0:T(8,128)S(1)} %get-tuple-element.59.tail_ref, ...), custom_call_target="tpu_custom_call" | custom-call | flops 603979776 | bytes 4000000 | tf_op jit(solution)/shard_map/pallas_call | solution.py:495
  67.4 1.7 %collective-permute-start.11 = (bf16[48,2048]{1,0:T(8,128)(2,1)S(1)}, bf16[48,2048]{1,0:T(8,128)(2,1)S(1)}, u32[]{:S(2)}, u32[]{:S(2)}) collective-permute-start(bf16[48,2048]{1,0:T(8,128)(2,1)S(1)} %get-tuple-element.62), channel_id=1, source_target_pairs={{0,1},{1,2},{2,3},{3,0},{4,5},{5,6},{6,7},{7,4},{8,9},{9,10},{10,1... | collective-permute-start | bytes 589832 | tf_op jit(solution)/shard_map/ppermute | solution.py:515
  69.1 2.9 %collective-permute-start.12 = (bf16[48,2048]{1,0:T(8,128)(2,1)S(1)}, bf16[48,2048]{1,0:T(8,128)(2,1)S(1)}, u32[]{:S(2)}, u32[]{:S(2)}) collective-permute-start(bf16[48,2048]{1,0:T(8,128)(2,1)S(1)} %get-tuple-element.63), channel_id=1, source_target_pairs={{0,2},{1,3},{2,0},{3,1},{4,6},{5,7},{6,4},{7,5},{8,10},{9,11},{10,... | collective-permute-start | bytes 589832 | tf_op jit(solution)/shard_map/ppermute | solution.py:515
  72.0 1.3 %collective-permute-start.13 = (bf16[48,2048]{1,0:T(8,128)(2,1)S(1)}, bf16[48,2048]{1,0:T(8,128)(2,1)S(1)}, u32[]{:S(2)}, u32[]{:S(2)}) collective-permute-start(bf16[48,2048]{1,0:T(8,128)(2,1)S(1)} %get-tuple-element.64), channel_id=1, source_target_pairs={{0,3},{1,0},{2,1},{3,2},{4,7},{5,4},{6,5},{7,6},{8,11},{9,8},{10,9... | collective-permute-start | bytes 589832 | tf_op jit(solution)/shard_map/ppermute | solution.py:515
  73.4 15.9 %all_to_all.5 = f32[8,3,4,256]{3,2,1,0:T(4,128)S(1)} all-to-all(f32[8,3,4,256]{3,2,1,0:T(4,128)S(1)} %broadcast_in_dim.3), channel_id=1, replica_groups={{0,32,64,96,128,160,192,224},{4,36,68,100,132,164,196,228},{8,40,72,104..., dimensions={0} | all-to-all | bytes 196608 | tf_op jit(solution)/shard_map/all_to_all | solution.py:523
  90.0 0.8 add_convert_fusion
  (34 shorter events, 2.7 us)
Async XLA Ops:
  0.6 9.2 %copy-start.6 = (s32[2,192]{1,0:T(2,128)S(1)}, s32[2,192]{1,0:T(2,128)}, u32[]{:S(2)}) copy-start(s32[2,192]{1,0:T(2,128)} %beta_ref.1) | copy-start | bytes 4612
  0.6 9.1 %copy-start.1 = (bf16[192,256]{1,0:T(8,128)(2,1)S(1)}, bf16[192,256]{1,0:T(8,128)(2,1)}, u32[]{:S(2)}) copy-start(bf16[192,256]{1,0:T(8,128)(2,1)} %grad_ref.5) | copy-start | bytes 294916
  0.7 9.1 %copy-start.4 = (f32[3,4,256]{2,1,0:T(4,128)S(1)}, f32[3,4,256]{2,1,0:T(4,128)}, u32[]{:S(2)}) copy-start(f32[3,4,256]{2,1,0:T(4,128)} %cw_ref.3) | copy-start | bytes 36868
  0.7 9.1 %copy-start.5 = (s32[2,192]{1,0:T(2,128)S(1)}, s32[2,192]{1,0:T(2,128)}, u32[]{:S(2)}) copy-start(s32[2,192]{1,0:T(2,128)} %gate_ref.1) | copy-start | bytes 4612
  4.4 5.4 %collective-permute-start = (f32[3,8,256]{2,1,0:T(8,128)}, f32[3,8,256]{2,1,0:T(8,128)S(1)}, u32[]{:S(2)}, u32[]{:S(2)}) collective-permute-start(f32[3,8,256]{2,1,0:T(8,128)} %get-tuple-element.35), channel_id=1, source_target_pairs={{0,4},{4,8},{8,12},{12,16},{16,20},{20,24},{24,28},{28,32},{32,36}... | collective-permute-start | bytes 73736 | tf_op jit(solution)/shard_map/ppermute | solution.py:445
  9.8 1.0 %copy-start.2 = (bf16[3,192,256]{2,1,0:T(8,128)(2,1)S(1)}, bf16[3,192,256]{2,1,0:T(8,128)(2,1)}, u32[]{:S(2)}) copy-start(bf16[3,192,256]{2,1,0:T(8,128)(2,1)} %get-tuple-element.34.proj_ref) | copy-start | bytes 884740
  15.8 36.9 %copy-start.3 = (bf16[3,192,256]{2,1,0:T(8,128)(2,1)S(1)}, bf16[3,192,256]{2,1,0:T(8,128)(2,1)}, u32[]{:S(2)}) copy-start(bf16[3,192,256]{2,1,0:T(8,128)(2,1)} %get-tuple-element.34.proj_ref) | copy-start | bytes 884740
  15.8 1.5 %collective-permute-start.1 = (f32[3,128,128]{2,1,0:T(8,128)S(1)}, f32[3,128,128]{2,1,0:T(8,128)S(1)}, u32[]{:S(2)}, u32[]{:S(2)}) collective-permute-start(f32[3,128,128]{2,1,0:T(8,128)S(1)} %get-tuple-element.37), channel_id=1, source_target_pairs={{0,4},{4,0},{8,12},{12,8},{16,20},{20,16},{24,28},{28,24},{32,36},... | collective-permute-start | bytes 589832 | tf_op jit(solution)/shard_map/ppermute | solution.py:423
  18.1 4.9 %collective-permute-start.2 = (bf16[3,128,128]{2,1,0:T(8,128)(2,1)S(1)}, bf16[3,128,128]{2,1,0:T(8,128)(2,1)S(1)}, u32[]{:S(2)}, u32[]{:S(2)}) collective-permute-start(bf16[3,128,128]{2,1,0:T(8,128)(2,1)S(1)} %shard_map.79.own_ref), channel_id=1, source_target_pairs={{0,8},{4,12},{8,16},{12,20},{16,24},{20,28},{24,0},{28,4},{32,40},... | collective-permute-start | bytes 294920 | tf_op jit(solution)/shard_map/ppermute | solution.py:430
  19.4 6.1 %collective-permute-start.3 = (bf16[3,128,128]{2,1,0:T(8,128)(2,1)S(1)}, bf16[3,128,128]{2,1,0:T(8,128)(2,1)S(1)}, u32[]{:S(2)}, u32[]{:S(2)}) collective-permute-start(bf16[3,128,128]{2,1,0:T(8,128)(2,1)S(1)} %shard_map.79.own_ref), channel_id=1, source_target_pairs={{0,16},{4,20},{8,24},{12,28},{16,0},{20,4},{24,8},{28,12},{32,48},... | collective-permute-start | bytes 294920 | tf_op jit(solution)/shard_map/ppermute | solution.py:430
  20.2 6.8 %collective-permute-start.4 = (bf16[3,128,128]{2,1,0:T(8,128)(2,1)S(1)}, bf16[3,128,128]{2,1,0:T(8,128)(2,1)S(1)}, u32[]{:S(2)}, u32[]{:S(2)}) collective-permute-start(bf16[3,128,128]{2,1,0:T(8,128)(2,1)S(1)} %shard_map.79.own_ref), channel_id=1, source_target_pairs={{0,24},{4,28},{8,0},{12,4},{16,8},{20,12},{24,16},{28,20},{32,56},... | collective-permute-start | bytes 294920 | tf_op jit(solution)/shard_map/ppermute | solution.py:430
  28.3 4.7 %collective-permute-start.5 = (bf16[3,128,128]{2,1,0:T(8,128)(2,1)S(1)}, bf16[3,128,128]{2,1,0:T(8,128)(2,1)S(1)}, u32[]{:S(2)}, u32[]{:S(2)}) collective-permute-start(bf16[3,128,128]{2,1,0:T(8,128)(2,1)S(1)} %get-tuple-element.38.own_ref), channel_id=1, source_target_pairs={{0,32},{4,36},{8,40},{12,44},{16,48},{20,52},{24,56},{28,60},{32,0... | collective-permute-start | bytes 294920 | tf_op jit(solution)/shard_map/ppermute | solution.py:423
  33.8 12.5 %collective-permute-start.6 = (bf16[2,128,128]{2,1,0:T(8,128)(2,1)S(1)}, bf16[2,128,128]{2,1,0:T(8,128)(2,1)S(1)}, u32[]{:S(2)}, u32[]{:S(2)}) collective-permute-start(bf16[2,128,128]{2,1,0:T(8,128)(2,1)S(1)} %get-tuple-element.39), channel_id=1, source_target_pairs={{0,64},{4,68},{8,72},{12,76},{16,80},{20,84},{24,88},{28,92},{32,9... | collective-permute-start | bytes 196616 | tf_op jit(solution)/shard_map/ppermute | solution.py:430
  37.1 9.3 %collective-permute-start.7 = (bf16[2,128,128]{2,1,0:T(8,128)(2,1)S(1)}, bf16[2,128,128]{2,1,0:T(8,128)(2,1)S(1)}, u32[]{:S(2)}, u32[]{:S(2)}) collective-permute-start(bf16[2,128,128]{2,1,0:T(8,128)(2,1)S(1)} %get-tuple-element.40), channel_id=1, source_target_pairs={{0,128},{4,132},{8,136},{12,140},{16,144},{20,148},{24,152},{28,15... | collective-permute-start | bytes 196616 | tf_op jit(solution)/shard_map/ppermute | solution.py:430
  42.5 6.1 %collective-permute-start.8 = (bf16[2,128,128]{2,1,0:T(8,128)(2,1)S(1)}, bf16[2,128,128]{2,1,0:T(8,128)(2,1)S(1)}, u32[]{:S(2)}, u32[]{:S(2)}) collective-permute-start(bf16[2,128,128]{2,1,0:T(8,128)(2,1)S(1)} %get-tuple-element.41), channel_id=1, source_target_pairs={{0,192},{4,196},{8,200},{12,204},{16,208},{20,212},{24,216},{28,22... | collective-permute-start | bytes 196616 | tf_op jit(solution)/shard_map/ppermute | solution.py:430
  50.0 2.7 %collective-permute-start.9 = (f32[2,128,128]{2,1,0:T(8,128)S(1)}, f32[2,128,128]{2,1,0:T(8,128)S(1)}, u32[]{:S(2)}, u32[]{:S(2)}) collective-permute-start(f32[2,128,128]{2,1,0:T(8,128)S(1)} %get-tuple-element.45), channel_id=1, source_target_pairs={{0,4},{4,0},{8,12},{12,8},{16,20},{20,16},{24,28},{28,24},{32,36},... | collective-permute-start | bytes 393224 | tf_op jit(solution)/shard_map/ppermute | solution.py:423
  52.7 12.2 %copy-start = (bf16[3,2048,256]{2,1,0:T(8,128)(2,1)S(1)}, bf16[3,2048,256]{2,1,0:T(8,128)(2,1)}, u32[]{:S(2)}) copy-start(bf16[3,2048,256]{2,1,0:T(8,128)(2,1)} %w_ref.3) | copy-start | bytes 9437188
  56.1 8.8 %collective-permute-start.10 = (f32[3,8,256]{2,1,0:T(8,128)S(1)}, f32[3,8,256]{2,1,0:T(8,128)S(1)}, u32[]{:S(2)}, u32[]{:S(2)}) collective-permute-start(f32[3,8,256]{2,1,0:T(8,128)S(1)} %get-tuple-element.60), channel_id=1, source_target_pairs={{4,0},{8,4},{12,8},{16,12},{20,16},{24,20},{28,24},{32,28},{36,32}... | collective-permute-start | bytes 73736 | tf_op jit(solution)/shard_map/ppermute | solution.py:491
  59.6 1.3 %collective-permute-start.14 = (f32[3,4,256]{2,1,0:T(4,128)S(1)}, f32[3,4,256]{2,1,0:T(4,128)S(1)}, u32[]{:S(2)}, u32[]{:S(2)}) collective-permute-start(f32[3,4,256]{2,1,0:T(4,128)S(1)} %get-tuple-element.65), channel_id=1, source_target_pairs={{0,4},{4,0},{8,12},{12,8},{16,20},{20,16},{24,28},{28,24},{32,36},... | collective-permute-start | bytes 36872 | tf_op jit(solution)/shard_map/ppermute | solution.py:423
  60.9 11.1 %collective-permute-start.15 = (f32[3,4,256]{2,1,0:T(4,128)S(1)}, f32[3,4,256]{2,1,0:T(4,128)S(1)}, u32[]{:S(2)}, u32[]{:S(2)}) collective-permute-start(f32[3,4,256]{2,1,0:T(4,128)S(1)} %add.35), channel_id=1, source_target_pairs={{0,16},{4,20},{8,24},{12,28},{16,0},{20,4},{24,8},{28,12},{32,48},... | collective-permute-start | bytes 36872 | tf_op jit(solution)/shard_map/ppermute | solution.py:430
  62.3 11.1 %collective-permute-start.16 = (f32[3,4,256]{2,1,0:T(4,128)S(1)}, f32[3,4,256]{2,1,0:T(4,128)S(1)}, u32[]{:S(2)}, u32[]{:S(2)}) collective-permute-start(f32[3,4,256]{2,1,0:T(4,128)S(1)} %add.35), channel_id=1, source_target_pairs={{0,8},{4,12},{8,16},{12,20},{16,24},{20,28},{24,0},{28,4},{32,40},... | collective-permute-start | bytes 36872 | tf_op jit(solution)/shard_map/ppermute | solution.py:430
  64.8 8.5 %collective-permute-start.17 = (f32[3,4,256]{2,1,0:T(4,128)S(1)}, f32[3,4,256]{2,1,0:T(4,128)S(1)}, u32[]{:S(2)}, u32[]{:S(2)}) collective-permute-start(f32[3,4,256]{2,1,0:T(4,128)S(1)} %add.35), channel_id=1, source_target_pairs={{0,24},{4,28},{8,0},{12,4},{16,8},{20,12},{24,16},{28,20},{32,56},... | collective-permute-start | bytes 36872 | tf_op jit(solution)/shard_map/ppermute | solution.py:430
  67.4 22.5 %collective-permute-start.11 = (bf16[48,2048]{1,0:T(8,128)(2,1)S(1)}, bf16[48,2048]{1,0:T(8,128)(2,1)S(1)}, u32[]{:S(2)}, u32[]{:S(2)}) collective-permute-start(bf16[48,2048]{1,0:T(8,128)(2,1)S(1)} %get-tuple-element.62), channel_id=1, source_target_pairs={{0,1},{1,2},{2,3},{3,0},{4,5},{5,6},{6,7},{7,4},{8,9},{9,10},{10,1... | collective-permute-start | bytes 589832 | tf_op jit(solution)/shard_map/ppermute | solution.py:515
  69.1 20.8 %collective-permute-start.12 = (bf16[48,2048]{1,0:T(8,128)(2,1)S(1)}, bf16[48,2048]{1,0:T(8,128)(2,1)S(1)}, u32[]{:S(2)}, u32[]{:S(2)}) collective-permute-start(bf16[48,2048]{1,0:T(8,128)(2,1)S(1)} %get-tuple-element.63), channel_id=1, source_target_pairs={{0,2},{1,3},{2,0},{3,1},{4,6},{5,7},{6,4},{7,5},{8,10},{9,11},{10,... | collective-permute-start | bytes 589832 | tf_op jit(solution)/shard_map/ppermute | solution.py:515
  72.0 17.9 %collective-permute-start.13 = (bf16[48,2048]{1,0:T(8,128)(2,1)S(1)}, bf16[48,2048]{1,0:T(8,128)(2,1)S(1)}, u32[]{:S(2)}, u32[]{:S(2)}) collective-permute-start(bf16[48,2048]{1,0:T(8,128)(2,1)S(1)} %get-tuple-element.64), channel_id=1, source_target_pairs={{0,3},{1,0},{2,1},{3,2},{4,7},{5,4},{6,5},{7,6},{8,11},{9,8},{10,9... | collective-permute-start | bytes 589832 | tf_op jit(solution)/shard_map/ppermute | solution.py:515

commit v2 on v1

--- a/solution.py
+++ b/solution.py
@@ -87,19 +87,15 @@
     return jax.ShapeDtypeStruct(s, d)
 
 
-def project_kernel(x_ref, w_ref, o_ref, tail_ref, x_held, w_held, sems):
-    copies = [pltpu.make_async_copy(x_ref, x_held, sems.at[3])]
+def edge_kernel(x_ref, o_ref):
+    o_ref[...] = x_ref[...]
+
+
+def project_kernel(x_ref, before_ref, w_ref, o_ref, halo_ref):
     for m in range(3):
-        copies.append(pltpu.make_async_copy(w_ref.at[m], w_held.at[m], sems.at[m]))
-    for copy in copies:
-        copy.start()
-    copies[0].wait()
-    rows = x_ref.shape[0]
-    for m in range(3):
-        copies[1 + m].wait()
-        value = dot(x_held[...], w_held[m], NN).astype(BF16)
-        o_ref[m] = value
-        tail_ref[m] = value[rows - 16 :].astype(F32)[8:]
+        o_ref[m] = dot(x_ref[...], w_ref[m], NN).astype(BF16)
+        halo = dot(before_ref[...], w_ref[m], NN).astype(BF16).astype(F32)
+        halo_ref[m] = halo
 
 
 def sigmoid(z):
@@ -430,19 +426,13 @@
         return lax.ppermute(block, "ctx", route)
 
 
-    projected, tail = pl.pallas_call(
+    last = call(edge_kernel, shape((8, width), BF16), flops=200_000_000_000)(inputs[rows - 8 :])
+    before = lax.ppermute(last, "ctx", [(i, i + 1) for i in range(n - 1)])
+    projected, halo = call(
         project_kernel,
-        in_specs=[pl.BlockSpec(memory_space=pl.ANY)] * 2,
-        out_specs=(pl.BlockSpec(memory_space=pltpu.VMEM),) * 2,
-        out_shape=(shape((3, rows, lanes), BF16), shape((3, 8, lanes))),
-        scratch_shapes=[
-            pltpu.VMEM((rows, width), BF16),
-            pltpu.VMEM((3, width, lanes), BF16),
-            pltpu.SemaphoreType.DMA((4,)),
-        ],
-        compiler_params=pltpu.CompilerParams(vmem_limit_bytes=66_500_000),
-    )(inputs, projection)
-    halo = lax.ppermute(tail, "ctx", [(i, i + 1) for i in range(n - 1)])
+        (shape((3, rows, lanes), BF16), shape((3, 8, lanes))),
+        flops=2_000_000_000,
+    )(inputs, before, projection)
     square = (2, rows, rows)
     tall = (2, rows, DK)
     triple = (3, DK, DK)
@@ -514,14 +504,15 @@
     for shift, block in enumerate(sends, 1):
         got = lax.ppermute(block, "head", [(i, (i + shift) % heads) for i in range(heads)])
         total = total + got.astype(F32)
-    zs = n // (2 * XS)
-    column = [[z * 2 * XS + i for z in range(zs)] for i in range(2 * XS)]
+
+    def around(taps, stride):
+        r1, r2, r3 = (turn(taps, stride, k) for k in (1, 2, 3))
+        return (taps + r2) + (r1 + r3)
+
     taps = taps + swap(taps, 1)
-    r1, r2, r3 = (turn(taps, 2, k) for k in (1, 2, 3))
-    taps = (taps + r2) + (r1 + r3)
-    taps = jnp.broadcast_to(taps, (zs,) + taps.shape)
-    taps = lax.all_to_all(taps, "ctx", 0, 0, axis_index_groups=column)
-    taps = jnp.sum(taps, 0)
+    taps = around(taps, 2)
+    taps = taps + swap(taps, 2 * XS)
+    taps = around(taps, 4 * XS)
     return (total.astype(BF16), taps)
 
 

time: 90.9 us -> 91.9 us (1.011)
  the two profiles are of different devices: /device:TPU:4 before, /device:TPU:2 now
where the time goes in v2:
time: 91.9 us; the launch traced here: 91.7 us
  starting transfers between devices  45.5 us (50%)
  waiting for transfers between devices  23.3 us (25%)
  Pallas kernels  18.8 us (20%)
  local copies, waits for them, and re-layouts  1.92 us (2%)
  other arithmetic  1.47 us (2%)
    ppermute x12, starting transfers between devices, turn(): return lax.ppermute(block, 'ctx', route)  30.8 us
    pallas_call x9, Pallas kernels, run(): pl.pallas_call(kernel, out_shape=out_shape, in_specs=specs, out_specs=jax...  16.2 us
    ppermute x5, waiting for transfers between devices, swap(): return lax.ppermute(block, 'ctx', [(i, i ^ bit) for i in range(n)])  7.95 us
    ppermute x12, waiting for transfers between devices, turn(): return lax.ppermute(block, 'ctx', route)  6.59 us
    ppermute x3, starting transfers between devices, body(): lax.ppermute(block, 'head', [(i, (i + shift) % heads) for i in range(head...  5.9 us
    ppermute x3, waiting for transfers between devices, body(): lax.ppermute(block, 'head', [(i, (i + shift) % heads) for i in range(head...  5.54 us
    ppermute x5, starting transfers between devices, swap(): return lax.ppermute(block, 'ctx', [(i, i ^ bit) for i in range(n)])  4.64 us
    ppermute x1, waiting for transfers between devices, body(): before = lax.ppermute(last, 'ctx', [(i, i + 1) for i in range(n - 1)])  3.18 us
  transfers between devices with their start and end apart: 22, of which 12 were waited for; matrix products, arithmetic and copies ran while one was open for 1% of the time, Pallas kernels for 5%

profile of v2, /device:TPU:2, one launch (start us, length us, event | category | flops | bytes accessed | tf_op | source)
XLA Modules:
  0.0 91.7 jit_solution(17208291169453921482)
XLA Ops:
  1.4 2.2 %collective-permute-start = (bf16[8,2048]{1,0:T(8,128)(2,1)S(1)}, bf16[8,2048]{1,0:T(8,128)(2,1)S(1)}, u32[]{:S(2)}, u32[]{:S(2)}) collective-permute-start(bf16[8,2048]{1,0:T(8,128)(2,1)S(1)} %shard_map.77), channel_id=1, source_target_pairs={{0,4},{4,8},{8,12},{12,16},{16,20},{20,24},{24,28},{28,32},{32,36}... | collective-permute-start | bytes 98312 | tf_op jit(solution)/shard_map/ppermute | solution.py:430
  3.7 3.2 %collective-permute-done.before_ref = bf16[8,2048]{1,0:T(8,128)(2,1)S(1)} collective-permute-done((bf16[8,2048]{1,0:T(8,128)(2,1)S(1)}, bf16[8,2048]{1,0:T(8,128)(2,1)S(1)}, u32[]{:S(2)}, u32[]{:S(2)}) %collective-permute-start) | collective-permute-done | bytes 32800 | tf_op jit(solution)/shard_map/ppermute | solution.py:430
  6.9 1.1 %copy-done.2 = bf16[192,2048]{1,0:T(8,128)(2,1)S(1)} copy-done((bf16[192,2048]{1,0:T(8,128)(2,1)S(1)}, bf16[192,2048]{1,0:T(8,128)(2,1)}, u32[]{:S(2)}) %copy-start.2) | copy-done | bytes 786456
  8.0 1.2 %shard_map.78 = (bf16[3,192,256]{2,1,0:T(8,128)(2,1)S(1)}, f32[3,8,256]{2,1,0:T(8,128)S(1)}) custom-call(bf16[192,2048]{1,0:T(8,128)(2,1)S(1)} %copy-done.2, bf16[8,2048]{1,0:T(8,128)(2,1)S(1)} %collective-permute-done.before_ref, bf16[3,2048,256]{2,1,0:T(8,128)(2,1)S(1)} %copy-done), custom_call_target="tpu_custom_call" | custom-call | flops 2000000000 | bytes 4000000 | tf_op jit(solution)/shard_map/pallas_call | solution.py:70
  9.3 5.0 %shard_map.79 = (f32[3,128,128]{2,1,0:T(8,128)S(1)}, f32[3,128,128]{2,1,0:T(8,128)S(1)}, f32[3,192,256]{2,1,0:T(8,128)S(1)}, f32[2,192,128]{2,1,0:T(8,128)S(1)},...) custom-call(s32[4]{0:T(128)S(1)} %pad_add_fusion.me_ref, ...), custom_call_target="tpu_custom_call" | custom-call | flops 2000000000 | bytes 4000000 | tf_op jit(solution)/shard_map/pallas_call | solution.py:70
  14.3 1.4 %collective-permute-done.1.recv_ref = f32[3,128,128]{2,1,0:T(8,128)S(1)} collective-permute-done((f32[3,128,128]{2,1,0:T(8,128)S(1)}, f32[3,128,128]{2,1,0:T(8,128)S(1)}, u32[]{:S(2)}, u32[]{:S(2)}) %collective-permute-start.1) | collective-permute-done | bytes 196640 | tf_op jit(solution)/shard_map/ppermute | solution.py:419
  16.6 1.6 %collective-permute-start.2 = (bf16[3,128,128]{2,1,0:T(8,128)(2,1)S(1)}, bf16[3,128,128]{2,1,0:T(8,128)(2,1)S(1)}, u32[]{:S(2)}, u32[]{:S(2)}) collective-permute-start(bf16[3,128,128]{2,1,0:T(8,128)(2,1)S(1)} %shard_map.80.own_ref), channel_id=1, source_target_pairs={{0,8},{4,12},{8,16},{12,20},{16,24},{20,28},{24,0},{28,4},{32,40},... | collective-permute-start | bytes 294920 | tf_op jit(solution)/shard_map/ppermute | solution.py:426
  18.9 2.5 %collective-permute-start.4 = (bf16[3,128,128]{2,1,0:T(8,128)(2,1)S(1)}, bf16[3,128,128]{2,1,0:T(8,128)(2,1)S(1)}, u32[]{:S(2)}, u32[]{:S(2)}) collective-permute-start(bf16[3,128,128]{2,1,0:T(8,128)(2,1)S(1)} %shard_map.80.own_ref), channel_id=1, source_target_pairs={{0,24},{4,28},{8,0},{12,4},{16,8},{20,12},{24,16},{28,20},{32,56},... | collective-permute-start | bytes 294920 | tf_op jit(solution)/shard_map/ppermute | solution.py:426
  21.5 3.8 %collective-permute-done.3.r2 = bf16[3,128,128]{2,1,0:T(8,128)(2,1)S(1)} collective-permute-done((bf16[3,128,128]{2,1,0:T(8,128)(2,1)S(1)}, bf16[3,128,128]{2,1,0:T(8,128)(2,1)S(1)}, u32[]{:S(2)}, u32[]{:S(2)}) %collective-permute-start.3) | collective-permute-done | bytes 98336 | tf_op jit(solution)/shard_map/ppermute | solution.py:426
  25.5 1.4 %shard_map.81 = (f32[2,128,128]{2,1,0:T(8,128)S(1)}, f32[2,128,128]{2,1,0:T(8,128)S(1)}, bf16[3,128,128]{2,1,0:T(8,128)(2,1)S(1)}) custom-call(s32[4]{0:T(128)S(1)} %pad_add_fusion.me_ref, bf16[3,128,128]{2,1,0:T(8,128)(2,1)S(1)} %shard_map.80.own_ref, bf16[3,128,128]{2,1,0:T(8,128)(2,1)S(1)} %collective-permute-done.2.r1, ...), custom_call_target="tpu_custom_call" | custom-call | bytes 4000000 | tf_op jit(solution)/shard_map/pallas_call | solution.py:70
  26.9 3.0 %collective-permute-start.5 = (bf16[3,128,128]{2,1,0:T(8,128)(2,1)S(1)}, bf16[3,128,128]{2,1,0:T(8,128)(2,1)S(1)}, u32[]{:S(2)}, u32[]{:S(2)}) collective-permute-start(bf16[3,128,128]{2,1,0:T(8,128)(2,1)S(1)} %get-tuple-element.38.own_ref), channel_id=1, source_target_pairs={{0,32},{4,36},{8,40},{12,44},{16,48},{20,52},{24,56},{28,60},{32,0... | collective-permute-start | bytes 294920 | tf_op jit(solution)/shard_map/ppermute | solution.py:419
  29.9 2.6 %collective-permute-done.5.recv_ref.near_ref = bf16[3,128,128]{2,1,0:T(8,128)(2,1)S(1)} collective-permute-done((bf16[3,128,128]{2,1,0:T(8,128)(2,1)S(1)}, bf16[3,128,128]{2,1,0:T(8,128)(2,1)S(1)}, u32[]{:S(2)}, u32[]{:S(2)}) %collective-permute-start.5) | collective-permute-done | bytes 98336 | tf_op jit(solution)/shard_map/ppermute | solution.py:419
  33.2 3.4 %collective-permute-start.6 = (bf16[2,128,128]{2,1,0:T(8,128)(2,1)S(1)}, bf16[2,128,128]{2,1,0:T(8,128)(2,1)S(1)}, u32[]{:S(2)}, u32[]{:S(2)}) collective-permute-start(bf16[2,128,128]{2,1,0:T(8,128)(2,1)S(1)} %get-tuple-element.39), channel_id=1, source_target_pairs={{0,64},{4,68},{8,72},{12,76},{16,80},{20,84},{24,88},{28,92},{32,9... | collective-permute-start | bytes 196616 | tf_op jit(solution)/shard_map/ppermute | solution.py:426
  36.7 5.4 %collective-permute-start.7 = (bf16[2,128,128]{2,1,0:T(8,128)(2,1)S(1)}, bf16[2,128,128]{2,1,0:T(8,128)(2,1)S(1)}, u32[]{:S(2)}, u32[]{:S(2)}) collective-permute-start(bf16[2,128,128]{2,1,0:T(8,128)(2,1)S(1)} %get-tuple-element.40), channel_id=1, source_target_pairs={{0,128},{4,132},{8,136},{12,140},{16,144},{20,148},{24,152},{28,15... | collective-permute-start | bytes 196616 | tf_op jit(solution)/shard_map/ppermute | solution.py:426
  42.1 3.7 %collective-permute-start.8 = (bf16[2,128,128]{2,1,0:T(8,128)(2,1)S(1)}, bf16[2,128,128]{2,1,0:T(8,128)(2,1)S(1)}, u32[]{:S(2)}, u32[]{:S(2)}) collective-permute-start(bf16[2,128,128]{2,1,0:T(8,128)(2,1)S(1)} %get-tuple-element.41), channel_id=1, source_target_pairs={{0,192},{4,196},{8,200},{12,204},{16,208},{20,212},{24,216},{28,22... | collective-permute-start | bytes 196616 | tf_op jit(solution)/shard_map/ppermute | solution.py:426
  45.8 2.3 %collective-permute-done.8.r3 = bf16[2,128,128]{2,1,0:T(8,128)(2,1)S(1)} collective-permute-done((bf16[2,128,128]{2,1,0:T(8,128)(2,1)S(1)}, bf16[2,128,128]{2,1,0:T(8,128)(2,1)S(1)}, u32[]{:S(2)}, u32[]{:S(2)}) %collective-permute-start.8) | collective-permute-done | bytes 65568 | tf_op jit(solution)/shard_map/ppermute | solution.py:426
  48.1 1.4 %shard_map.83 = (f32[2,128,128]{2,1,0:T(8,128)S(1)}, f32[2,128,128]{2,1,0:T(8,128)S(1)}) custom-call(s32[4]{0:T(128)S(1)} %pad_add_fusion.me_ref, bf16[2,128,128]{2,1,0:T(8,128)(2,1)S(1)} %collective-permute-done.6.r1, bf16[2,128,128]{2,1,0:T(8,128)(2,1)S(1)} %collective-permute-done.7.r2, bf16[2,128,128]{2,1,0:T(8,128)(2,1)S(1)} %collective-permute-done.8.r3, ...), custom_call_target="tpu_custom_call" | custom-call | bytes 4000000 | tf_op jit(solution)/shard_map/pallas_call | solution.py:70
  49.8 2.4 %shard_map.84 = (f32[2,192,128]{2,1,0:T(8,128)S(1)}, f32[2,192,128]{2,1,0:T(8,128)S(1)}) custom-call(f32[2,192,192]{2,1,0:T(8,128)S(1)} %get-tuple-element.53.p_ref, f32[2,192,192]{2,1,0:T(8,128)S(1)} %get-tuple-element.54.a_ref, f32[2,3,64,64]{3,2,1,0:T(8,128)S(1)} %get-tuple-element.55.t_ref, f32[2,192,128]{2,1,0:T(8,128)S(1)} %get-tuple-element.48.k_ref, ...), custom_call_target="tpu_custom_call" | custom-call | flops 500000000 | bytes 4000000 | tf_op jit(solution)/shard_map/pallas_call | solution.py:70
  52.2 3.4 %shard_map.85 = (bf16[3,192,256]{2,1,0:T(8,128)(2,1)S(1)}, f32[3,16,256]{2,1,0:T(8,128)S(1)}, f32[3,8,256]{2,1,0:T(8,128)S(1)}, f32[3,4,256]{2,1,0:T(4,128)S(1)}) custom-call(s32[4]{0:T(128)S(1)} %pad_add_fusion.me_ref, f32[2,128,128]{2,1,0:T(8,128)S(1)} %get-tuple-element.44.own_ref, f32[2,128,128]{2,1,0:T(8,128)S(1)} %collective-permute-done.9.recv_ref, ...), custom_call_target="tpu_custom_call" | custom-call | flops 2000000000 | bytes 4000000 | tf_op jit(solution)/shard_map/pallas_call | solution.py:70
  57.0 2.9 %collective-permute-start.15 = (f32[3,4,256]{2,1,0:T(4,128)S(1)}, f32[3,4,256]{2,1,0:T(4,128)S(1)}, u32[]{:S(2)}, u32[]{:S(2)}) collective-permute-start(f32[3,4,256]{2,1,0:T(4,128)S(1)} %add.47), channel_id=1, source_target_pairs={{0,16},{4,20},{8,24},{12,28},{16,0},{20,4},{24,8},{28,12},{32,48},... | collective-permute-start | bytes 36872 | tf_op jit(solution)/shard_map/ppermute | solution.py:426
  60.3 1.6 %collective-permute-start.17 = (f32[3,4,256]{2,1,0:T(4,128)S(1)}, f32[3,4,256]{2,1,0:T(4,128)S(1)}, u32[]{:S(2)}, u32[]{:S(2)}) collective-permute-start(f32[3,4,256]{2,1,0:T(4,128)S(1)} %add.47), channel_id=1, source_target_pairs={{0,24},{4,28},{8,0},{12,4},{16,8},{20,12},{24,16},{28,20},{32,56},... | collective-permute-start | bytes 36872 | tf_op jit(solution)/shard_map/ppermute | solution.py:426
  61.9 1.9 %collective-permute-start.10 = (f32[3,8,256]{2,1,0:T(8,128)S(1)}, f32[3,8,256]{2,1,0:T(8,128)S(1)}, u32[]{:S(2)}, u32[]{:S(2)}) collective-permute-start(f32[3,8,256]{2,1,0:T(8,128)S(1)} %get-tuple-element.60), channel_id=1, source_target_pairs={{4,0},{8,4},{12,8},{16,12},{20,16},{24,20},{28,24},{32,28},{36,32}... | collective-permute-start | bytes 73736 | tf_op jit(solution)/shard_map/ppermute | solution.py:481
  64.7 3.1 %collective-permute-done.18 = f32[3,4,256]{2,1,0:T(4,128)S(1)} collective-permute-done((f32[3,4,256]{2,1,0:T(4,128)S(1)}, f32[3,4,256]{2,1,0:T(4,128)S(1)}, u32[]{:S(2)}, u32[]{:S(2)}) %collective-permute-start.18) | collective-permute-done | bytes 12320 | tf_op jit(solution)/shard_map/ppermute | solution.py:419
  67.8 4.4 %collective-permute-start.19 = (f32[3,4,256]{2,1,0:T(4,128)S(1)}, f32[3,4,256]{2,1,0:T(4,128)S(1)}, u32[]{:S(2)}, u32[]{:S(2)}) collective-permute-start(f32[3,4,256]{2,1,0:T(4,128)S(1)} %add.51), channel_id=1, source_target_pairs={{0,128},{4,132},{8,136},{12,140},{16,144},{20,148},{24,152},{28,15... | collective-permute-start | bytes 36872 | tf_op jit(solution)/shard_map/ppermute | solution.py:426
  72.2 2.4 %collective-permute-start.20 = (f32[3,4,256]{2,1,0:T(4,128)S(1)}, f32[3,4,256]{2,1,0:T(4,128)S(1)}, u32[]{:S(2)}, u32[]{:S(2)}) collective-permute-start(f32[3,4,256]{2,1,0:T(4,128)S(1)} %add.51), channel_id=1, source_target_pairs={{0,64},{4,68},{8,72},{12,76},{16,80},{20,84},{24,88},{28,92},{32,9... | collective-permute-start | bytes 36872 | tf_op jit(solution)/shard_map/ppermute | solution.py:426
  74.5 1.8 %collective-permute-start.21 = (f32[3,4,256]{2,1,0:T(4,128)S(1)}, f32[3,4,256]{2,1,0:T(4,128)S(1)}, u32[]{:S(2)}, u32[]{:S(2)}) collective-permute-start(f32[3,4,256]{2,1,0:T(4,128)S(1)} %add.51), channel_id=1, source_target_pairs={{0,192},{4,196},{8,200},{12,204},{16,208},{20,212},{24,216},{28,22... | collective-permute-start | bytes 36872 | tf_op jit(solution)/shard_map/ppermute | solution.py:426
  76.3 2.6 %shard_map.86 = (f32[48,2048]{1,0:T(8,128)S(1)}, bf16[48,2048]{1,0:T(8,128)(2,1)S(1)}, bf16[48,2048]{1,0:T(8,128)(2,1)S(1)}, bf16[48,2048]{1,0:T(8,128)(2,1)S(1)}) custom-call(s32[4]{0:T(128)S(1)} %pad_add_fusion.me_ref, bf16[3,192,256]{2,1,0:T(8,128)(2,1)S(1)} %get-tuple-element.58.grad_ref, f32[3,16,256]{2,1,0:T(8,128)S(1)} %get-tuple-element.59.tail_ref, ...), custom_call_target="tpu_custom_call" | custom-call | flops 603979776 | bytes 4000000 | tf_op jit(solution)/shard_map/pallas_call | solution.py:485
  78.9 1.7 %collective-permute-start.11 = (bf16[48,2048]{1,0:T(8,128)(2,1)S(1)}, bf16[48,2048]{1,0:T(8,128)(2,1)S(1)}, u32[]{:S(2)}, u32[]{:S(2)}) collective-permute-start(bf16[48,2048]{1,0:T(8,128)(2,1)S(1)} %get-tuple-element.62), channel_id=1, source_target_pairs={{0,1},{1,2},{2,3},{3,0},{4,5},{5,6},{6,7},{7,4},{8,9},{9,10},{10,1... | collective-permute-start | bytes 589832 | tf_op jit(solution)/shard_map/ppermute | solution.py:505
  80.6 2.9 %collective-permute-start.12 = (bf16[48,2048]{1,0:T(8,128)(2,1)S(1)}, bf16[48,2048]{1,0:T(8,128)(2,1)S(1)}, u32[]{:S(2)}, u32[]{:S(2)}) collective-permute-start(bf16[48,2048]{1,0:T(8,128)(2,1)S(1)} %get-tuple-element.63), channel_id=1, source_target_pairs={{0,2},{1,3},{2,0},{3,1},{4,6},{5,7},{6,4},{7,5},{8,10},{9,11},{10,... | collective-permute-start | bytes 589832 | tf_op jit(solution)/shard_map/ppermute | solution.py:505
  83.5 1.3 %collective-permute-start.13 = (bf16[48,2048]{1,0:T(8,128)(2,1)S(1)}, bf16[48,2048]{1,0:T(8,128)(2,1)S(1)}, u32[]{:S(2)}, u32[]{:S(2)}) collective-permute-start(bf16[48,2048]{1,0:T(8,128)(2,1)S(1)} %get-tuple-element.64), channel_id=1, source_target_pairs={{0,3},{1,0},{2,1},{3,2},{4,7},{5,4},{6,5},{7,6},{8,11},{9,8},{10,9... | collective-permute-start | bytes 589832 | tf_op jit(solution)/shard_map/ppermute | solution.py:505
  85.4 2.0 %collective-permute-done.11 = bf16[48,2048]{1,0:T(8,128)(2,1)S(1)} collective-permute-done((bf16[48,2048]{1,0:T(8,128)(2,1)S(1)}, bf16[48,2048]{1,0:T(8,128)(2,1)S(1)}, u32[]{:S(2)}, u32[]{:S(2)}) %collective-permute-start.11) | collective-permute-done | bytes 196640 | tf_op jit(solution)/shard_map/ppermute | solution.py:505
  87.4 3.5 %collective-permute-done.12 = bf16[48,2048]{1,0:T(8,128)(2,1)S(1)} collective-permute-done((bf16[48,2048]{1,0:T(8,128)(2,1)S(1)}, bf16[48,2048]{1,0:T(8,128)(2,1)S(1)}, u32[]{:S(2)}, u32[]{:S(2)}) %collective-permute-start.12) | collective-permute-done | bytes 196640 | tf_op jit(solution)/shard_map/ppermute | solution.py:505
  (41 shorter events, 7.9 us)
Async XLA Ops:
  1.4 5.5 %copy-start = (bf16[3,2048,256]{2,1,0:T(8,128)(2,1)S(1)}, bf16[3,2048,256]{2,1,0:T(8,128)(2,1)}, u32[]{:S(2)}) copy-start(bf16[3,2048,256]{2,1,0:T(8,128)(2,1)} %w_ref.3) | copy-start | bytes 9437188
  1.4 5.5 %collective-permute-start = (bf16[8,2048]{1,0:T(8,128)(2,1)S(1)}, bf16[8,2048]{1,0:T(8,128)(2,1)S(1)}, u32[]{:S(2)}, u32[]{:S(2)}) collective-permute-start(bf16[8,2048]{1,0:T(8,128)(2,1)S(1)} %shard_map.77), channel_id=1, source_target_pairs={{0,4},{4,8},{8,12},{12,16},{16,20},{20,24},{24,28},{28,32},{32,36}... | collective-permute-start | bytes 98312 | tf_op jit(solution)/shard_map/ppermute | solution.py:430
  3.7 5.5 %copy-start.1 = (bf16[192,256]{1,0:T(8,128)(2,1)S(1)}, bf16[192,256]{1,0:T(8,128)(2,1)}, u32[]{:S(2)}) copy-start(bf16[192,256]{1,0:T(8,128)(2,1)} %grad_ref.5) | copy-start | bytes 294916
  6.9 1.1 %copy-start.2 = (bf16[192,2048]{1,0:T(8,128)(2,1)S(1)}, bf16[192,2048]{1,0:T(8,128)(2,1)}, u32[]{:S(2)}) copy-start(bf16[192,2048]{1,0:T(8,128)(2,1)} %x_ref.1) | copy-start | bytes 2359300
  8.0 1.2 %copy-start.3 = (f32[3,4,256]{2,1,0:T(4,128)S(1)}, f32[3,4,256]{2,1,0:T(4,128)}, u32[]{:S(2)}) copy-start(f32[3,4,256]{2,1,0:T(4,128)} %cw_ref.3) | copy-start | bytes 36868
  8.0 1.2 %copy-start.4 = (s32[2,192]{1,0:T(2,128)S(1)}, s32[2,192]{1,0:T(2,128)}, u32[]{:S(2)}) copy-start(s32[2,192]{1,0:T(2,128)} %gate_ref.1) | copy-start | bytes 4612
  8.0 1.2 %copy-start.5 = (s32[2,192]{1,0:T(2,128)S(1)}, s32[2,192]{1,0:T(2,128)}, u32[]{:S(2)}) copy-start(s32[2,192]{1,0:T(2,128)} %beta_ref.1) | copy-start | bytes 4612
  14.2 1.5 %collective-permute-start.1 = (f32[3,128,128]{2,1,0:T(8,128)S(1)}, f32[3,128,128]{2,1,0:T(8,128)S(1)}, u32[]{:S(2)}, u32[]{:S(2)}) collective-permute-start(f32[3,128,128]{2,1,0:T(8,128)S(1)} %get-tuple-element.37), channel_id=1, source_target_pairs={{0,4},{4,0},{8,12},{12,8},{16,20},{20,16},{24,28},{28,24},{32,36},... | collective-permute-start | bytes 589832 | tf_op jit(solution)/shard_map/ppermute | solution.py:419
  16.6 4.9 %collective-permute-start.2 = (bf16[3,128,128]{2,1,0:T(8,128)(2,1)S(1)}, bf16[3,128,128]{2,1,0:T(8,128)(2,1)S(1)}, u32[]{:S(2)}, u32[]{:S(2)}) collective-permute-start(bf16[3,128,128]{2,1,0:T(8,128)(2,1)S(1)} %shard_map.80.own_ref), channel_id=1, source_target_pairs={{0,8},{4,12},{8,16},{12,20},{16,24},{20,28},{24,0},{28,4},{32,40},... | collective-permute-start | bytes 294920 | tf_op jit(solution)/shard_map/ppermute | solution.py:426
  18.1 7.2 %collective-permute-start.3 = (bf16[3,128,128]{2,1,0:T(8,128)(2,1)S(1)}, bf16[3,128,128]{2,1,0:T(8,128)(2,1)S(1)}, u32[]{:S(2)}, u32[]{:S(2)}) collective-permute-start(bf16[3,128,128]{2,1,0:T(8,128)(2,1)S(1)} %shard_map.80.own_ref), channel_id=1, source_target_pairs={{0,16},{4,20},{8,24},{12,28},{16,0},{20,4},{24,8},{28,12},{32,48},... | collective-permute-start | bytes 294920 | tf_op jit(solution)/shard_map/ppermute | solution.py:426
  18.9 6.7 %collective-permute-start.4 = (bf16[3,128,128]{2,1,0:T(8,128)(2,1)S(1)}, bf16[3,128,128]{2,1,0:T(8,128)(2,1)S(1)}, u32[]{:S(2)}, u32[]{:S(2)}) collective-permute-start(bf16[3,128,128]{2,1,0:T(8,128)(2,1)S(1)} %shard_map.80.own_ref), channel_id=1, source_target_pairs={{0,24},{4,28},{8,0},{12,4},{16,8},{20,12},{24,16},{28,20},{32,56},... | collective-permute-start | bytes 294920 | tf_op jit(solution)/shard_map/ppermute | solution.py:426
  26.9 5.6 %collective-permute-start.5 = (bf16[3,128,128]{2,1,0:T(8,128)(2,1)S(1)}, bf16[3,128,128]{2,1,0:T(8,128)(2,1)S(1)}, u32[]{:S(2)}, u32[]{:S(2)}) collective-permute-start(bf16[3,128,128]{2,1,0:T(8,128)(2,1)S(1)} %get-tuple-element.38.own_ref), channel_id=1, source_target_pairs={{0,32},{4,36},{8,40},{12,44},{16,48},{20,52},{24,56},{28,60},{32,0... | collective-permute-start | bytes 294920 | tf_op jit(solution)/shard_map/ppermute | solution.py:419
  33.2 12.6 %collective-permute-start.6 = (bf16[2,128,128]{2,1,0:T(8,128)(2,1)S(1)}, bf16[2,128,128]{2,1,0:T(8,128)(2,1)S(1)}, u32[]{:S(2)}, u32[]{:S(2)}) collective-permute-start(bf16[2,128,128]{2,1,0:T(8,128)(2,1)S(1)} %get-tuple-element.39), channel_id=1, source_target_pairs={{0,64},{4,68},{8,72},{12,76},{16,80},{20,84},{24,88},{28,92},{32,9... | collective-permute-start | bytes 196616 | tf_op jit(solution)/shard_map/ppermute | solution.py:426
  36.7 9.1 %collective-permute-start.7 = (bf16[2,128,128]{2,1,0:T(8,128)(2,1)S(1)}, bf16[2,128,128]{2,1,0:T(8,128)(2,1)S(1)}, u32[]{:S(2)}, u32[]{:S(2)}) collective-permute-start(bf16[2,128,128]{2,1,0:T(8,128)(2,1)S(1)} %get-tuple-element.40), channel_id=1, source_target_pairs={{0,128},{4,132},{8,136},{12,140},{16,144},{20,148},{24,152},{28,15... | collective-permute-start | bytes 196616 | tf_op jit(solution)/shard_map/ppermute | solution.py:426
  42.1 6.0 %collective-permute-start.8 = (bf16[2,128,128]{2,1,0:T(8,128)(2,1)S(1)}, bf16[2,128,128]{2,1,0:T(8,128)(2,1)S(1)}, u32[]{:S(2)}, u32[]{:S(2)}) collective-permute-start(bf16[2,128,128]{2,1,0:T(8,128)(2,1)S(1)} %get-tuple-element.41), channel_id=1, source_target_pairs={{0,192},{4,196},{8,200},{12,204},{16,208},{20,212},{24,216},{28,22... | collective-permute-start | bytes 196616 | tf_op jit(solution)/shard_map/ppermute | solution.py:426
  49.5 2.7 %collective-permute-start.9 = (f32[2,128,128]{2,1,0:T(8,128)S(1)}, f32[2,128,128]{2,1,0:T(8,128)S(1)}, u32[]{:S(2)}, u32[]{:S(2)}) collective-permute-start(f32[2,128,128]{2,1,0:T(8,128)S(1)} %get-tuple-element.45), channel_id=1, source_target_pairs={{0,4},{4,0},{8,12},{12,8},{16,20},{20,16},{24,28},{28,24},{32,36},... | collective-permute-start | bytes 393224 | tf_op jit(solution)/shard_map/ppermute | solution.py:419
  55.5 1.4 %collective-permute-start.14 = (f32[3,4,256]{2,1,0:T(4,128)S(1)}, f32[3,4,256]{2,1,0:T(4,128)S(1)}, u32[]{:S(2)}, u32[]{:S(2)}) collective-permute-start(f32[3,4,256]{2,1,0:T(4,128)S(1)} %get-tuple-element.65), channel_id=1, source_target_pairs={{0,4},{4,0},{8,12},{12,8},{16,20},{20,16},{24,28},{28,24},{32,36},... | collective-permute-start | bytes 36872 | tf_op jit(solution)/shard_map/ppermute | solution.py:419
  57.0 6.8 %collective-permute-start.15 = (f32[3,4,256]{2,1,0:T(4,128)S(1)}, f32[3,4,256]{2,1,0:T(4,128)S(1)}, u32[]{:S(2)}, u32[]{:S(2)}) collective-permute-start(f32[3,4,256]{2,1,0:T(4,128)S(1)} %add.47), channel_id=1, source_target_pairs={{0,16},{4,20},{8,24},{12,28},{16,0},{20,4},{24,8},{28,12},{32,48},... | collective-permute-start | bytes 36872 | tf_op jit(solution)/shard_map/ppermute | solution.py:426
  59.8 4.0 %collective-permute-start.16 = (f32[3,4,256]{2,1,0:T(4,128)S(1)}, f32[3,4,256]{2,1,0:T(4,128)S(1)}, u32[]{:S(2)}, u32[]{:S(2)}) collective-permute-start(f32[3,4,256]{2,1,0:T(4,128)S(1)} %add.47), channel_id=1, source_target_pairs={{0,8},{4,12},{8,16},{12,20},{16,24},{20,28},{24,0},{28,4},{32,40},... | collective-permute-start | bytes 36872 | tf_op jit(solution)/shard_map/ppermute | solution.py:426
  60.3 3.7 %collective-permute-start.17 = (f32[3,4,256]{2,1,0:T(4,128)S(1)}, f32[3,4,256]{2,1,0:T(4,128)S(1)}, u32[]{:S(2)}, u32[]{:S(2)}) collective-permute-start(f32[3,4,256]{2,1,0:T(4,128)S(1)} %add.47), channel_id=1, source_target_pairs={{0,24},{4,28},{8,0},{12,4},{16,8},{20,12},{24,16},{28,20},{32,56},... | collective-permute-start | bytes 36872 | tf_op jit(solution)/shard_map/ppermute | solution.py:426
  61.9 14.5 %collective-permute-start.10 = (f32[3,8,256]{2,1,0:T(8,128)S(1)}, f32[3,8,256]{2,1,0:T(8,128)S(1)}, u32[]{:S(2)}, u32[]{:S(2)}) collective-permute-start(f32[3,8,256]{2,1,0:T(8,128)S(1)} %get-tuple-element.60), channel_id=1, source_target_pairs={{4,0},{8,4},{12,8},{16,12},{20,16},{24,20},{28,24},{32,28},{36,32}... | collective-permute-start | bytes 73736 | tf_op jit(solution)/shard_map/ppermute | solution.py:481
  64.0 3.8 %collective-permute-start.18 = (f32[3,4,256]{2,1,0:T(4,128)S(1)}, f32[3,4,256]{2,1,0:T(4,128)S(1)}, u32[]{:S(2)}, u32[]{:S(2)}) collective-permute-start(f32[3,4,256]{2,1,0:T(4,128)S(1)} %add_add_fusion.1), channel_id=1, source_target_pairs={{0,32},{4,36},{8,40},{12,44},{16,48},{20,52},{24,56},{28,60},{32,0... | collective-permute-start | bytes 36872 | tf_op jit(solution)/shard_map/ppermute | solution.py:419
  67.8 15.7 %collective-permute-start.19 = (f32[3,4,256]{2,1,0:T(4,128)S(1)}, f32[3,4,256]{2,1,0:T(4,128)S(1)}, u32[]{:S(2)}, u32[]{:S(2)}) collective-permute-start(f32[3,4,256]{2,1,0:T(4,128)S(1)} %add.51), channel_id=1, source_target_pairs={{0,128},{4,132},{8,136},{12,140},{16,144},{20,148},{24,152},{28,15... | collective-permute-start | bytes 36872 | tf_op jit(solution)/shard_map/ppermute | solution.py:426
  72.2 12.6 %collective-permute-start.20 = (f32[3,4,256]{2,1,0:T(4,128)S(1)}, f32[3,4,256]{2,1,0:T(4,128)S(1)}, u32[]{:S(2)}, u32[]{:S(2)}) collective-permute-start(f32[3,4,256]{2,1,0:T(4,128)S(1)} %add.51), channel_id=1, source_target_pairs={{0,64},{4,68},{8,72},{12,76},{16,80},{20,84},{24,88},{28,92},{32,9... | collective-permute-start | bytes 36872 | tf_op jit(solution)/shard_map/ppermute | solution.py:426
  74.5 10.3 %collective-permute-start.21 = (f32[3,4,256]{2,1,0:T(4,128)S(1)}, f32[3,4,256]{2,1,0:T(4,128)S(1)}, u32[]{:S(2)}, u32[]{:S(2)}) collective-permute-start(f32[3,4,256]{2,1,0:T(4,128)S(1)} %add.51), channel_id=1, source_target_pairs={{0,192},{4,196},{8,200},{12,204},{16,208},{20,212},{24,216},{28,22... | collective-permute-start | bytes 36872 | tf_op jit(solution)/shard_map/ppermute | solution.py:426
  78.9 8.5 %collective-permute-start.11 = (bf16[48,2048]{1,0:T(8,128)(2,1)S(1)}, bf16[48,2048]{1,0:T(8,128)(2,1)S(1)}, u32[]{:S(2)}, u32[]{:S(2)}) collective-permute-start(bf16[48,2048]{1,0:T(8,128)(2,1)S(1)} %get-tuple-element.62), channel_id=1, source_target_pairs={{0,1},{1,2},{2,3},{3,0},{4,5},{5,6},{6,7},{7,4},{8,9},{9,10},{10,1... | collective-permute-start | bytes 589832 | tf_op jit(solution)/shard_map/ppermute | solution.py:505
  80.6 10.4 %collective-permute-start.12 = (bf16[48,2048]{1,0:T(8,128)(2,1)S(1)}, bf16[48,2048]{1,0:T(8,128)(2,1)S(1)}, u32[]{:S(2)}, u32[]{:S(2)}) collective-permute-start(bf16[48,2048]{1,0:T(8,128)(2,1)S(1)} %get-tuple-element.63), channel_id=1, source_target_pairs={{0,2},{1,3},{2,0},{3,1},{4,6},{5,7},{6,4},{7,5},{8,10},{9,11},{10,... | collective-permute-start | bytes 589832 | tf_op jit(solution)/shard_map/ppermute | solution.py:505
  83.5 7.5 %collective-permute-start.13 = (bf16[48,2048]{1,0:T(8,128)(2,1)S(1)}, bf16[48,2048]{1,0:T(8,128)(2,1)S(1)}, u32[]{:S(2)}, u32[]{:S(2)}) collective-permute-start(bf16[48,2048]{1,0:T(8,128)(2,1)S(1)} %get-tuple-element.64), channel_id=1, source_target_pairs={{0,3},{1,0},{2,1},{3,2},{4,7},{5,4},{6,5},{7,6},{8,11},{9,8},{10,9... | collective-permute-start | bytes 589832 | tf_op jit(solution)/shard_map/ppermute | solution.py:505
